TPU v7x, 32 devices: a whole 2x2x4 slice. The times are simulated.
32 devices in a mesh: groups: 2 (over y), blk: 4 (over z), tok: 4 (over x, core).
Axes of the slice: x: 2, y: 2, z: 4, core: 2. Of those that a mesh axis runs over, the one named last changes fastest.
Arguments:
- inputs: bfloat16 [12288, 2048], P(('groups', 'tok'), 'blk'), parts along dimension 0, may hold values from -6 to 6
- targets: bfloat16 [12288, 2048], P(('groups', 'tok'), 'blk'), parts along dimension 0, may hold values from -6 to 6
- left_factor: bfloat16 [16, 256, 256], P(('groups', 'blk')), parts along dimension 0, may hold values from -0.375 to 0.375
- right_factor: bfloat16 [16, 256, 256], P(('groups', 'blk')), parts along dimension 0, may hold values from -0.375 to 0.375
Outputs:
- grad_left: float32 [16, 256, 256], P(('groups', 'blk'), 'tok'), parts along dimension 0
- grad_right: float32 [16, 256, 256], P(('groups', 'blk'), 'tok'), parts along dimension 0
There are 2 independent parts, one for each index of `groups`. A program takes and returns all parts, laid end to end along the dimension named above; each array names one. Nothing has to cross between parts.
All inputs are finite; a program needn't handle non-finite values.
Results may differ from a plain program's by a relative error of at most 0.0015.
Values may be sent and summed in bfloat16 or wider, within the bound.
No kernel may reach another device: no remote copies, remote signals or barrier semaphores. Data moves between devices by JAX's collectives and lax.ppermute only.
A program may use at most 64 MiB of HBM per device.

v0:
```python
import jax
import jax.numpy as jnp
from jax import lax
from jax.sharding import PartitionSpec as P


def on_device(inputs, targets, left_factor, right_factor):
    local_blocks = left_factor.shape[0]
    block_width = left_factor.shape[1]
    tok_rows = inputs.shape[0]
    peer_count = lax.axis_size("blk")
    all_blocks = local_blocks * peer_count
    stride_len = block_width // all_blocks
    shaped = inputs.reshape(tok_rows, local_blocks, block_width)
    first_out = jnp.einsum(
        "tki,kji->kjt", shaped, left_factor, preferred_element_type=jnp.float32
    ).astype(jnp.bfloat16)
    outgoing = first_out.reshape(local_blocks, peer_count, local_blocks, stride_len, tok_rows)
    right_view = right_factor.reshape(local_blocks, block_width, all_blocks, stride_len)
    arrived = lax.all_to_all(outgoing, "blk", split_axis=1, concat_axis=0, tiled=True)
    mixed_part = arrived[:, 0]
    student_part = jnp.einsum(
        "gokm,kgmt->got", right_view, mixed_part, preferred_element_type=jnp.float32
    )
    student_four = student_part[:, :, None, :]
    student = student_four[:, :, 0, :]
    truth = targets.reshape(tok_rows, local_blocks, block_width).transpose(1, 2, 0)
    error_rows = (student - truth.astype(jnp.float32)).astype(jnp.bfloat16)
    inverse_rows = jnp.float32(1.0 / tok_rows)
    term_right = jnp.einsum(
        "got,kgmt->gokm", error_rows, mixed_part, preferred_element_type=jnp.float32
    ).reshape(local_blocks, block_width, block_width)
    backward_in = jnp.einsum(
        "gokm,got->kgmt", right_view, error_rows, preferred_element_type=jnp.float32
    ).astype(jnp.bfloat16)
    returned = lax.all_to_all(backward_in, "blk", split_axis=0, concat_axis=1, tiled=True)
    back_first = returned.reshape(local_blocks, block_width, tok_rows)
    term_left = jnp.einsum("kjt,tki->kji", back_first, shaped, preferred_element_type=jnp.float32)
    summed_left, summed_right = (
        lax.psum_scatter(term_left, "tok", scatter_dimension=1, tiled=True),
        lax.psum_scatter(term_right, "tok", scatter_dimension=1, tiled=True),
    )
    return (summed_left * inverse_rows, summed_right * inverse_rows)


def solution(mesh):
    in_specs = (
        P(("groups", "tok"), "blk"),
        P(("groups", "tok"), "blk"),
        P(("groups", "blk"), None, None),
        P(("groups", "blk"), None, None),
    )
    out_specs = (P(("groups", "blk"), "tok", None), P(("groups", "blk"), "tok", None))
    return jax.shard_map(
        on_device, mesh=mesh, in_specs=in_specs, out_specs=out_specs, check_vma=False
    )
```

profile of v0, /device:TPU:21, one launch (start us, length us, event | category | flops | bytes accessed | tf_op | source)
XLA Modules:
  0.0 131.7 jit_solution(9672742158649602140)
XLA Ops:
  7.2 0.0 copy-start
  7.2 0.9 copy-done
  8.1 2.0 %convolution_convert_fusion = bf16[2,256,1536]{2,1,0:T(8,128)(2,1)S(1)} fusion(bf16[2,256,256]{2,1,0:T(8,128)(2,1)S(1)} %copy-done, bf16[192,2,8,256]{3,2,1,0:T(8,128)(2,1)} %bitcast.57), kind=kOutput, calls=%fused_computation.3 | convolution fusion | flops 403439616 | bytes 3407872 | tf_op jit(solution)/shard_map/tki,kji->kjt/dot_general | solution.py:15
  10.1 1.3 copy.26
  11.4 0.0 copy-start.4
  11.4 4.8 %all-to-all-start = ((bf16[2,4,2,32,1536]{4,3,2,0,1:T(8,128)(2,1)}), bf16[2,4,2,32,1536]{4,3,2,0,1:T(8,128)(2,1)S(1)}, u32[]{:S(2)}, u32[]{:S(2)}) async-start(bf16[2,4,2,32,1536]{4,3,2,0,1:T(8,128)(2,1)} %copy.26), calls=%async_computation | async-start | bytes 3145728 | tf_op jit(solution)/shard_map/all_to_all | solution.py:20
  16.2 0.0 copy-done.4
  16.2 0.8 copy.28
  17.1 1.7 %copy.29 = bf16[1536,512]{0,1:T(8,128)(2,1)S(1)} copy(bf16[1536,512]{1,0:T(8,128)(2,1)} %param.5) | data formatting | bytes 3145728 | tf_op args[1]
  18.8 2.0 %copy.30 = f32[1536,2,256]{2,0,1:T(8,128)} copy(bf16[1536,2,256]{0,2,1:T(8,128)(2,1)S(1)} %bitcast.53) | data formatting | bytes 4718592 | tf_op jit(solution)/shard_map/convert_element_type | solution.py:28
  20.8 28.9 %all-to-all-done = bf16[2,4,2,32,1536]{4,3,2,0,1:T(8,128)(2,1)S(1)} async-done(((bf16[2,4,2,32,1536]{4,3,2,0,1:T(8,128)(2,1)}), bf16[2,4,2,32,1536]{4,3,2,0,1:T(8,128)(2,1)S(1)}, u32[]{:S(2)}, u32[]{:S(2)}) %all-to-all-start) | async-done | bytes 1572896 | tf_op jit(solution)/shard_map/all_to_all | solution.py:20
  49.7 0.0 copy-start.1
  49.7 0.1 copy.27
  49.8 0.0 copy-start.2
  49.8 2.3 %copy-done.1 = f32[1536,2,256]{2,0,1:T(8,128)S(1)} copy-done((f32[1536,2,256]{2,0,1:T(8,128)S(1)}, f32[1536,2,256]{2,0,1:T(8,128)}, u32[]{:S(2)}) %copy-start.1) | copy-done | bytes 3145752
  52.1 0.0 copy-start.5
  52.1 1.8 %fusion.1 = bf16[2,256,1536]{1,2,0:T(8,128)(2,1)S(1)} fusion(f32[1536,2,256]{2,0,1:T(8,128)S(1)} %copy-done.1, bf16[8,2,32,1536]{3,2,0,1:T(8,128)(2,1)S(1)} %bitcast.54, bf16[2,256,8,32]{1,3,2,0:T(8,128)(2,1)} %bitcast.60), kind=kOutput, calls=%fused_computation.2 | convolution fusion | flops 404226048 | bytes 6553600 | tf_op jit(solution)/shard_map/gokm,kgmt->got/dot_general | solution.py:22
  53.9 0.0 copy-done.2
  53.9 0.0 copy-done.5
  53.9 0.6 fusion.9
  54.5 0.2 convert_bitcast_fusion
  54.8 1.3 copy.32
  56.0 6.5 %all-to-all-start.1 = ((bf16[8,2,32,1536]{3,2,1,0:T(8,128)(2,1)}), bf16[8,2,32,1536]{3,2,1,0:T(8,128)(2,1)S(1)}, u32[]{:S(2)}, u32[]{:S(2)}) async-start(bf16[8,2,32,1536]{3,2,1,0:T(8,128)(2,1)} %copy.32), calls=%async_computation.1 | async-start | bytes 3145728 | tf_op jit(solution)/shard_map/all_to_all | solution.py:36
  62.6 0.0 reduce-scatter.5.cloned.1.call-start
  62.6 2.8 %fusion.5 = f32[2,256,8,32]{1,3,2,0:T(8,128)} fusion(bf16[8,2,32,1536]{3,2,0,1:T(8,128)(2,1)} %bitcast.55, bf16[2,256,1536]{1,2,0:T(8,128)(2,1)S(1)} %fusion.1), kind=kOutput, calls=%fused_computation.7 | convolution fusion | flops 402653184 | bytes 3670016 | tf_op jit(solution)/shard_map/got,kgmt->gokm/dot_general | solution.py:30
  65.4 2.0 %copy.36 = f32[2,256,256]{2,1,0:T(8,128)} copy(f32[2,256,256]{1,2,0:T(8,128)} %bitcast.59) | data formatting | bytes 1048576 | tf_op jit(solution)/shard_map/reshape | solution.py:32
  67.4 0.0 reduce-scatter.5.cloned.1.call-update
  67.4 0.0 reduce-scatter.3.cloned.1.call-start
  67.5 28.6 %all-to-all-done.1 = bf16[8,2,32,1536]{3,2,1,0:T(8,128)(2,1)S(1)} async-done(((bf16[8,2,32,1536]{3,2,1,0:T(8,128)(2,1)}), bf16[8,2,32,1536]{3,2,1,0:T(8,128)(2,1)S(1)}, u32[]{:S(2)}, u32[]{:S(2)}) %all-to-all-start.1) | async-done | bytes 1572896 | tf_op jit(solution)/shard_map/all_to_all | solution.py:36
  96.0 0.0 copy-start.3
  96.0 0.1 copy.33
  96.1 1.3 copy-done.3
  97.4 1.4 %fusion.2 = f32[2,256,256]{2,1,0:T(8,128)} fusion(bf16[2,256,1536]{2,1,0:T(8,128)(2,1)S(1)} %bitcast.56, bf16[192,2,8,256]{3,2,1,0:T(8,128)(2,1)S(1)} %bitcast.58), kind=kOutput, calls=%fused_computation.4 | convolution fusion | flops 402653184 | bytes 3670016 | tf_op jit(solution)/shard_map/kjt,tki->kji/dot_general | solution.py:38
  98.8 0.0 reduce-scatter.3.cloned.1.call-update
  98.8 0.0 reduce-scatter.5.cloned.1.call-done
  98.9 1.6 %broadcast_multiply_fusion = f32[2,64,256]{2,1,0:T(8,128)} fusion(f32[2,64,256]{2,1,0:T(8,128)} %reduce-scatter.5.cloned.1.call-done), kind=kLoop, calls=%fused_computation.12 | loop fusion | flops 32768 | bytes 262144 | tf_op jit(solution)/shard_map/mul | solution.py:43
  100.4 22.8 %reduce-scatter.3.cloned.1.call-done = f32[2,64,256]{2,1,0:T(8,128)} async-done(((f32[2,256,256]{2,1,0:T(8,128)}), f32[2,64,256]{2,1,0:T(8,128)}) %reduce-scatter.3.cloned.1.call-update) | async-done | bytes 131088 | tf_op jit(solution)/shard_map/reduce_scatter | solution.py:40
  123.3 1.6 %broadcast_multiply_fusion.1 = f32[2,64,256]{2,1,0:T(8,128)} fusion(f32[2,64,256]{2,1,0:T(8,128)} %reduce-scatter.3.cloned.1.call-done), kind=kLoop, calls=%fused_computation.13 | loop fusion | flops 32768 | bytes 262144 | tf_op jit(solution)/shard_map/mul | solution.py:43
Async XLA Ops:
  7.2 1.0 copy-start
  11.4 4.8 %copy-start.4 = (bf16[2,256,256]{2,1,0:T(8,128)(2,1)S(1)}, bf16[2,256,256]{2,1,0:T(8,128)(2,1)}, u32[]{:S(2)}) copy-start(bf16[2,256,256]{2,1,0:T(8,128)(2,1)} %param.7) | copy-start | bytes 786436
  11.4 38.3 %all-to-all-start = ((bf16[2,4,2,32,1536]{4,3,2,0,1:T(8,128)(2,1)}), bf16[2,4,2,32,1536]{4,3,2,0,1:T(8,128)(2,1)S(1)}, u32[]{:S(2)}, u32[]{:S(2)}) async-start(bf16[2,4,2,32,1536]{4,3,2,0,1:T(8,128)(2,1)} %copy.26), calls=%async_computation | async-start | bytes 3145728 | tf_op jit(solution)/shard_map/all_to_all | solution.py:20
  49.7 2.5 %copy-start.1 = (f32[1536,2,256]{2,0,1:T(8,128)S(1)}, f32[1536,2,256]{2,0,1:T(8,128)}, u32[]{:S(2)}) copy-start(f32[1536,2,256]{2,0,1:T(8,128)} %copy.30) | copy-start | bytes 9437188
  49.8 4.1 %copy-start.2 = (bf16[4,2,1,2,32,1536]{5,4,1,0,3,2:T(8,128)(2,1)}, bf16[4,2,1,2,32,1536]{5,4,1,0,3,2:T(8,128)(2,1)S(1)}, u32[]{:S(2)}) copy-start(bf16[4,2,1,2,32,1536]{5,4,1,0,3,2:T(8,128)(2,1)S(1)} %copy.27) | copy-start | bytes 4718596
  52.1 1.8 %copy-start.5 = (bf16[2,256,256]{2,1,0:T(8,128)(2,1)S(1)}, bf16[2,256,256]{2,1,0:T(8,128)(2,1)}, u32[]{:S(2)}) copy-start(bf16[2,256,256]{2,1,0:T(8,128)(2,1)} %param.7) | copy-start | bytes 786436
  56.0 40.0 %all-to-all-start.1 = ((bf16[8,2,32,1536]{3,2,1,0:T(8,128)(2,1)}), bf16[8,2,32,1536]{3,2,1,0:T(8,128)(2,1)S(1)}, u32[]{:S(2)}, u32[]{:S(2)}) async-start(bf16[8,2,32,1536]{3,2,1,0:T(8,128)(2,1)} %copy.32), calls=%async_computation.1 | async-start | bytes 3145728 | tf_op jit(solution)/shard_map/all_to_all | solution.py:36
  62.6 36.3 %reduce-scatter.5.cloned.1.call-start = ((), (), s32[]{:S(2)}) async-start(), calls=%async_computation.5 | async-start | bytes 655360 | tf_op jit(solution)/shard_map/reduce_scatter | solution.py:41
  67.4 55.8 %reduce-scatter.3.cloned.1.call-start = ((), (), s32[]{:S(2)}) async-start(), calls=%async_computation.4 | async-start | bytes 655360 | tf_op jit(solution)/shard_map/reduce_scatter | solution.py:40
  96.0 1.4 %copy-start.3 = (bf16[1536,512]{1,0:T(8,128)(2,1)S(1)}, bf16[1536,512]{1,0:T(8,128)(2,1)}, u32[]{:S(2)}) copy-start(bf16[1536,512]{1,0:T(8,128)(2,1)} %param.4) | copy-start | bytes 4718596
Sparse Core Ops, SparseCore 0:
  67.5 23.6 reduce-scatter.4
  98.9 24.2 reduce-scatter.2
where the time goes:
time: 134 us; the launch traced here: 132 us
  waiting for transfers between devices  80.3 us (60%)
  between operations  14.1 us (11%)
  local copies, waits for them, and re-layouts  14 us (10%)
  starting transfers between devices  11.3 us (8%)
  matrix products  8.53 us (6%)
  other arithmetic  3.34 us (2%)
    all_to_all x1, waiting for transfers between devices, on_device(): lax.all_to_all(outgoing, 'blk', split_axis=1, concat_axis=0, tiled=True)  28.9 us
    all_to_all x1, waiting for transfers between devices, on_device(): lax.all_to_all(backward_in, 'blk', split_axis=0, concat_axis=1, tiled=True)  28.6 us
    reduce_scatter x1, waiting for transfers between devices, on_device(): lax.psum_scatter(term_left, 'tok', scatter_dimension=1, tiled=True)  22.8 us
    unnamed x14, local copies, waits for them, and re-layouts  7.16 us
    all_to_all x1, starting transfers between devices, on_device(): lax.all_to_all(backward_in, 'blk', split_axis=0, concat_axis=1, tiled=True)  6.53 us
    all_to_all x1, starting transfers between devices, on_device(): lax.all_to_all(outgoing, 'blk', split_axis=1, concat_axis=0, tiled=True)  4.78 us
    mul x2, other arithmetic, on_device(): return (summed_left * inverse_rows, summed_right * inverse_rows)  3.14 us
    dot_general x1, matrix products, on_device(): jnp.einsum('got,kgmt->gokm', error_rows, mixed_part, preferred_element_ty...  2.78 us
  transfers between devices with their start and end apart: 4, of which 3 were waited for; matrix products, arithmetic and copies ran while one was open for 9% of the time, Pallas kernels for 0%

commit v1 on v0

v1 whole, which is shorter than its diff:
```python
import functools

import jax
import jax.numpy as jnp
from jax import lax
from jax.experimental import pallas as pl
from jax.experimental.pallas import tpu as pltpu
from jax.sharding import PartitionSpec as P

F32, BF16 = jnp.float32, jnp.bfloat16
NT = (((1,), (1,)), ((), ()))
NN = (((1,), (0,)), ((), ()))
TN = (((0,), (0,)), ((), ()))


def dot(a, b, dims):
    return lax.dot_general(a, b, dims, preferred_element_type=F32)


def after(value, *others):
    return lax.optimization_barrier((value, others))[0]


def params():
    return pltpu.CompilerParams(vmem_limit_bytes=48 << 20)


def whole(shape):
    return pl.BlockSpec(shape, lambda i: (0,) * len(shape))


def forward_kernel(peers, left_ref, x_ref, *refs):
    outs, left_rel = refs[:peers], refs[peers]
    blocks, width = left_ref.shape[0], left_ref.shape[1]
    rows = width // peers
    step = rows // blocks
    me = lax.axis_index("blk")

    @pl.when(pl.program_id(0) == 0)
    def _():
        for d in range(peers):
            at = pl.multiple_of((me ^ d) * rows, rows)
            for k in range(blocks):
                left_rel[k, d * rows : (d + 1) * rows, :] = left_ref[k, pl.ds(at, rows), :]

    for k in range(blocks):
        first = dot(left_rel[k], x_ref[:, k * width : (k + 1) * width], NT).astype(BF16)
        for d in range(peers):
            for g in range(blocks):
                low = d * rows + g * step
                outs[d][g, k * step : (k + 1) * step, :] = first[low : low + step]


def forward(left, x, peers, start, size, tile):
    blocks, width, _ = left.shape
    rows = width // peers
    base = start // tile
    return pl.pallas_call(
        functools.partial(forward_kernel, peers),
        grid=(size // tile,),
        in_specs=[
            whole(left.shape),
            pl.BlockSpec((tile, x.shape[1]), lambda i: (base + i, 0)),
        ],
        out_specs=[pl.BlockSpec((blocks, rows, tile), lambda i: (0, 0, i))] * peers,
        out_shape=[jax.ShapeDtypeStruct((blocks, rows, size), BF16)] * peers,
        scratch_shapes=[pltpu.VMEM(left.shape, BF16)],
        compiler_params=params(),
        name="forward",
    )(left, x)


def middle_kernel(peers, toks, has_prior, last, right_ref, targets_ref, *refs):
    pieces = refs[:peers]
    refs = refs[peers:]
    prior = refs[0] if has_prior else None
    refs = refs[1:] if has_prior else refs
    backs = refs[:peers]
    if last:
        terms, mixed, back, total = refs[peers : peers + toks], *refs[peers + toks :]
    else:
        total, mixed, back = refs[peers:]
    blocks, width = right_ref.shape[0], right_ref.shape[1]
    rows = width // peers
    step = rows // blocks
    me = lax.axis_index("blk")
    i = pl.program_id(0)

    @pl.when(i == 0)
    def _():
        total[...] = prior[...] if has_prior else jnp.zeros_like(total)

    for d in range(peers):
        at = pl.multiple_of((me ^ d) * rows, rows)
        for g in range(blocks):
            mixed[g, pl.ds(at, rows), :] = pieces[d][g]
    for g in range(blocks):
        truth = targets_ref[:, g * width : (g + 1) * width].astype(F32).T
        error = (dot(right_ref[g], mixed[g], NN) - truth).astype(BF16)
        back[g] = dot(right_ref[g], error, TN).astype(BF16)
        total[g] += dot(error, mixed[g], NT)
    own = lax.axis_index("tok")
    for s in range(peers):
        at = pl.multiple_of((own ^ s) * rows, rows)
        for g in range(blocks):
            part = back[g, pl.ds(at, rows), :]
            for k in range(blocks):
                backs[s][k, g * step : (g + 1) * step, :] = part[k * step : (k + 1) * step]
    if last:

        @pl.when(i == pl.num_programs(0) - 1)
        def _():
            size = width // toks
            for s in range(toks):
                at = pl.multiple_of((own ^ s) * size, size)
                terms[s][...] = total[:, pl.ds(at, size), :]


def middle(right, targets, pieces, prior, peers, toks, start, size, tile, last):
    blocks, width, _ = right.shape
    rows = width // peers
    base = start // tile
    piece = pl.BlockSpec((blocks, rows, tile), lambda i: (0, 0, i))
    grad = (blocks, width, width)
    term = (blocks, width // toks, width)
    extra = [] if prior is None else [prior]
    tail = [term] * toks if last else [grad]
    scratch = [pltpu.VMEM((blocks, width, tile), BF16)] * 2
    if last:
        scratch = scratch + [pltpu.VMEM(grad, F32)]
    return pl.pallas_call(
        functools.partial(middle_kernel, peers, toks, prior is not None, last),
        grid=(size // tile,),
        in_specs=[
            whole(right.shape),
            pl.BlockSpec((tile, targets.shape[1]), lambda i: (base + i, 0)),
        ]
        + [piece] * peers
        + [whole(grad)] * len(extra),
        out_specs=[piece] * peers + [whole(t) for t in tail],
        out_shape=[jax.ShapeDtypeStruct((blocks, rows, size), BF16)] * peers
        + [jax.ShapeDtypeStruct(t, F32) for t in tail],
        scratch_shapes=scratch,
        compiler_params=params(),
        name="middle",
    )(right, targets, *pieces, *extra)


def left_kernel(toks, scale, has_prior, *refs):
    pieces = refs[:toks]
    rows_ref = refs[toks]
    prior = refs[toks + 1] if has_prior else None
    out = refs[-1]
    blocks = out.shape[0]
    width = out.shape[2]
    mine = lax.axis_index("blk") ^ lax.axis_index("tok")

    def slot(r):
        at, bit = 0, 1
        while bit < toks:
            at = 2 * at + (r // bit) % 2
            bit *= 2
        return at

    for k in range(blocks):
        total = prior[k] if has_prior else None
        for s in range(toks):
            rows = rows_ref[slot(mine ^ s), :, k * width : (k + 1) * width]
            term = dot(pieces[s][k], rows, NN)
            total = term if total is None else total + term
        out[k] = total * scale


def left_rows(pieces, gathered, prior, toks, scale, start, size, width):
    blocks, rows, _ = pieces[0].shape
    shape = (blocks, rows, width)
    extra = [] if prior is None else [prior]
    at = start // size
    return pl.pallas_call(
        functools.partial(left_kernel, toks, scale, prior is not None),
        grid=(1,),
        in_specs=[whole(pieces[0].shape)] * toks
        + [pl.BlockSpec((toks, size, gathered.shape[2]), lambda i: (0, at, 0))]
        + [whole(shape)] * len(extra),
        out_specs=whole(shape),
        out_shape=jax.ShapeDtypeStruct(shape, F32),
        compiler_params=params(),
        name="left_rows",
    )(*pieces, gathered, *extra)


def on_device(inputs, targets, left_factor, right_factor):
    width = left_factor.shape[1]
    tok_rows = inputs.shape[0]
    peers = lax.axis_size("blk")
    toks = lax.axis_size("tok")
    inverse_rows = 1.0 / tok_rows
    chunks = ((0, tok_rows * 2 // 3), (tok_rows * 2 // 3, tok_rows // 3))
    tile = tok_rows // 3

    def over(axis, size, d):
        return functools.partial(
            lax.ppermute, axis_name=axis, perm=[(j, j ^ d) for j in range(size)]
        )

    def homeward(s):
        pairs = [
            (b * toks + t, (t ^ s) * toks + b) for b in range(peers) for t in range(toks)
        ]
        return functools.partial(lax.ppermute, axis_name=("blk", "tok"), perm=pairs)

    arrived = []
    left = left_factor
    for start, size in chunks:
        pieces = forward(left, inputs, peers, start, size, tile)
        left = after(left_factor, *pieces)
        order = sorted(range(1, peers), reverse=True)
        got = {d: over("blk", peers, d)(pieces[d]) for d in order}
        arrived.append([pieces[0]] + [got[d] for d in range(1, peers)])

    gathered = after(inputs, *pieces)[None]
    hop = toks // 2
    crossed = over("tok", toks, hop)(gathered)

    prior, sent = None, []
    for c, (start, size) in enumerate(chunks):
        last = c == len(chunks) - 1
        res = middle(
            right_factor, targets, arrived[c], prior, peers, toks, start, size, tile, last
        )
        backs, rest = res[:peers], res[peers:]
        prior = rest[0]
        sent.append(backs)
    terms = rest

    home = [[homeward(s)(backs[s]) for s in range(toks)] for backs in sent]
    while hop:
        gathered = jnp.concatenate([gathered, after(crossed, *terms)])
        hop //= 2
        if hop:
            crossed = over("tok", toks, hop)(gathered)

    terms = after(tuple(terms), home[0][0])
    summed_right = terms[0]
    for s in range(1, toks):
        summed_right = summed_right + over("tok", toks, s)(terms[s])

    total = None
    for c, (start, size) in enumerate(chunks):
        scale = inverse_rows if c == len(chunks) - 1 else 1.0
        total = left_rows(home[c], gathered, total, toks, scale, start, size, width)
    return (total, summed_right * jnp.float32(inverse_rows))


def solution(mesh):
    in_specs = (
        P(("groups", "tok"), "blk"),
        P(("groups", "tok"), "blk"),
        P(("groups", "blk"), None, None),
        P(("groups", "blk"), None, None),
    )
    out_specs = (P(("groups", "blk"), "tok", None), P(("groups", "blk"), "tok", None))
    return jax.shard_map(
        on_device, mesh=mesh, in_specs=in_specs, out_specs=out_specs, check_vma=False
    )
```

time: 134 us -> 107 us (0.80); the launches traced: 132 us -> 106 us
  waiting for transfers between devices: 80.3 us -> 62.2 us
  between operations: 14.1 us -> 0.76 us
  local copies, waits for them, and re-layouts: 14 us -> 0.95 us
  starting transfers between devices: 11.3 us -> 23.6 us
  Pallas kernels: 0 us -> 12.2 us
  matrix products: 8.53 us -> 0 us
  other arithmetic: 3.34 us -> 6.61 us
    ppermute x0 -> x19, waiting for transfers between devices: none -> 62.2 us  [the longest x8 30.7 us: on_device(): home = [[homeward(s)(backs[s]) for s in range(toks)] for backs in sent]]
    all_to_all x2 -> x0, waiting for transfers between devices: 57.4 us -> none  [the longest x1 28.9 us: on_device(): lax.all_to_all(outgoing, 'blk', split_axis=1, concat_axis=0, tiled=True)]
    ppermute x0 -> x19, starting transfers between devices: none -> 23.6 us  [the longest x8 10.4 us: on_device(): home = [[homeward(s)(backs[s]) for s in range(toks)] for backs in sent]]
    reduce_scatter x2 -> x0, waiting for transfers between devices: 22.9 us -> none  [the longest x1 22.8 us: on_device(): lax.psum_scatter(term_left, 'tok', scatter_dimension=1, tiled=True)]
    pallas_call x0 -> x6, Pallas kernels: none -> 12.2 us  [the longest x2 5.75 us: left_rows(): pl.pallas_call(functools.partial(left_kernel, toks, scale, prior is not N...]
    all_to_all x2 -> x0, starting transfers between devices: 11.3 us -> none  [the longest x1 6.53 us: on_device(): lax.all_to_all(backward_in, 'blk', split_axis=0, concat_axis=1, tiled=True)]
    dot_general x4 -> x0, matrix products: 7.91 us -> none  [the longest x1 2.78 us: on_device(): jnp.einsum('got,kgmt->gokm', error_rows, mixed_part, preferred_element_ty...]
    unnamed x14 -> x6, local copies, waits for them, and re-layouts: 7.16 us -> 0.95 us
  transfers between devices with their start and end apart: 4 -> 19, of which waited for: 3 -> 11; matrix products, arithmetic and copies ran while one was open for 9% -> 5% of each run, Pallas kernels for 0% -> 6%
where the time goes in v1:
time: 107 us; the launch traced here: 106 us
  waiting for transfers between devices  62.2 us (58%)
  starting transfers between devices  23.6 us (22%)
  Pallas kernels  12.2 us (11%)
  other arithmetic  6.61 us (6%)
    ppermute x8, waiting for transfers between devices, on_device(): home = [[homeward(s)(backs[s]) for s in range(toks)] for backs in sent]  30.7 us
    ppermute x6, waiting for transfers between devices, on_device(): got = {d: over('blk', peers, d)(pieces[d]) for d in order}  26.3 us
    ppermute x8, starting transfers between devices, on_device(): home = [[homeward(s)(backs[s]) for s in range(toks)] for backs in sent]  10.4 us
    ppermute x6, starting transfers between devices, on_device(): got = {d: over('blk', peers, d)(pieces[d]) for d in order}  7.28 us
    concatenate x2, other arithmetic, on_device(): gathered = jnp.concatenate([gathered, after(crossed, *terms)])  5.92 us
    pallas_call x2, Pallas kernels, left_rows(): pl.pallas_call(functools.partial(left_kernel, toks, scale, prior is not N...  5.75 us
    ppermute x3, waiting for transfers between devices, on_device(): summed_right = summed_right + over('tok', toks, s)(terms[s])  5.25 us
    ppermute x2, starting transfers between devices, on_device(): crossed = over('tok', toks, hop)(gathered)  3.75 us
  transfers between devices with their start and end apart: 19, of which 11 were waited for; matrix products, arithmetic and copies ran while one was open for 5% of the time, Pallas kernels for 6%

profile of v1, /device:TPU:21, one launch (start us, length us, event | category | flops | bytes accessed | tf_op | source)
XLA Modules:
  0.0 106.3 jit_solution(11279308148398869372)
XLA Ops:
  0.6 0.0 copy-start.1
  0.6 0.9 copy-done.1
  1.6 0.0 copy-start
  1.6 0.0 copy-start.2
  1.6 2.0 %forward.2 = (bf16[2,64,1024]{2,1,0:T(8,128)(2,1)S(1)}, bf16[2,64,1024]{2,1,0:T(8,128)(2,1)S(1)}, bf16[2,64,1024]{2,1,0:T(8,128)(2,1)S(1)}, bf16[2,64,1024]{2,1,0:T(8,128)(2,1)S(1)}) custom-call(bf16[2,256,256]{2,1,0:T(8,128)(2,1)S(1)} %copy-done.1, bf16[1536,512]{1,0:T(8,128)(2,1)} %x_ref.3), custom_call_target="tpu_custom_call" | custom-call | tf_op jit(solution)/shard_map/forward/pallas_call | solution.py:58
  3.6 1.4 %forward.3 = (bf16[2,64,512]{2,1,0:T(8,128)(2,1)S(1)}, bf16[2,64,512]{2,1,0:T(8,128)(2,1)S(1)}, bf16[2,64,512]{2,1,0:T(8,128)(2,1)S(1)}, bf16[2,64,512]{2,1,0:T(8,128)(2,1)S(1)}) custom-call(bf16[2,256,256]{2,1,0:T(8,128)(2,1)S(1)} %copy-done.1, bf16[1536,512]{1,0:T(8,128)(2,1)} %x_ref.3), custom_call_target="tpu_custom_call" | custom-call | tf_op jit(solution)/shard_map/forward/pallas_call | solution.py:58
  4.9 1.3 %collective-permute-start.10 = (bf16[1,1536,512]{2,1,0:T(8,128)(2,1)}, bf16[1,1536,512]{2,1,0:T(8,128)(2,1)S(1)}, u32[]{:S(2)}, u32[]{:S(2)}) collective-permute-start(bf16[1,1536,512]{2,1,0:T(8,128)(2,1)} %bitcast), channel_id=1, source_target_pairs={{0,2},{1,3},{2,0},{3,1},{4,6},{5,7},{6,4},{7,5},{8,10},{9,11},{10,... | collective-permute-start | bytes 4718600 | tf_op jit(solution)/shard_map/ppermute | solution.py:223
  6.2 1.3 %collective-permute-start.3 = (bf16[2,64,1024]{2,1,0:T(8,128)(2,1)S(1)}, bf16[2,64,1024]{2,1,0:T(8,128)(2,1)S(1)}, u32[]{:S(2)}, u32[]{:S(2)}) collective-permute-start(bf16[2,64,1024]{2,1,0:T(8,128)(2,1)S(1)} %get-tuple-element.32), channel_id=1, source_target_pairs={{0,4},{4,0},{8,12},{12,8},{1,5},{5,1},{9,13},{13,9},{2,6},{6,2},{1... | collective-permute-start | bytes 786440 | tf_op jit(solution)/shard_map/ppermute | solution.py:218
  7.5 0.1 collective-permute-start.4
  7.6 1.3 %collective-permute-start.5 = (bf16[2,64,1024]{2,1,0:T(8,128)(2,1)S(1)}, bf16[2,64,1024]{2,1,0:T(8,128)(2,1)S(1)}, u32[]{:S(2)}, u32[]{:S(2)}) collective-permute-start(bf16[2,64,1024]{2,1,0:T(8,128)(2,1)S(1)} %get-tuple-element.34), channel_id=1, source_target_pairs={{0,12},{4,8},{8,4},{12,0},{1,13},{5,9},{9,5},{13,1},{2,14},{6,10},... | collective-permute-start | bytes 786440 | tf_op jit(solution)/shard_map/ppermute | solution.py:218
  8.9 2.2 %collective-permute-start = (bf16[2,64,512]{2,1,0:T(8,128)(2,1)S(1)}, bf16[2,64,512]{2,1,0:T(8,128)(2,1)S(1)}, u32[]{:S(2)}, u32[]{:S(2)}) collective-permute-start(bf16[2,64,512]{2,1,0:T(8,128)(2,1)S(1)} %get-tuple-element.37), channel_id=1, source_target_pairs={{0,4},{4,0},{8,12},{12,8},{1,5},{5,1},{9,13},{13,9},{2,6},{6,2},{1... | collective-permute-start | bytes 393224 | tf_op jit(solution)/shard_map/ppermute | solution.py:218
  11.1 5.5 %collective-permute-done.3.refs_1_ = bf16[2,64,1024]{2,1,0:T(8,128)(2,1)S(1)} collective-permute-done((bf16[2,64,1024]{2,1,0:T(8,128)(2,1)S(1)}, bf16[2,64,1024]{2,1,0:T(8,128)(2,1)S(1)}, u32[]{:S(2)}, u32[]{:S(2)}) %collective-permute-start.3) | collective-permute-done | bytes 262176 | tf_op jit(solution)/shard_map/ppermute | solution.py:218
  16.6 1.1 %collective-permute-start.1 = (bf16[2,64,512]{2,1,0:T(8,128)(2,1)S(1)}, bf16[2,64,512]{2,1,0:T(8,128)(2,1)S(1)}, u32[]{:S(2)}, u32[]{:S(2)}) collective-permute-start(bf16[2,64,512]{2,1,0:T(8,128)(2,1)S(1)} %get-tuple-element.38), channel_id=1, source_target_pairs={{0,8},{4,12},{8,0},{12,4},{1,9},{5,13},{9,1},{13,5},{2,10},{6,14},... | collective-permute-start | bytes 393224 | tf_op jit(solution)/shard_map/ppermute | solution.py:218
  17.7 0.9 collective-permute-done.4.refs_2_
  18.6 1.3 %collective-permute-start.2 = (bf16[2,64,512]{2,1,0:T(8,128)(2,1)S(1)}, bf16[2,64,512]{2,1,0:T(8,128)(2,1)S(1)}, u32[]{:S(2)}, u32[]{:S(2)}) collective-permute-start(bf16[2,64,512]{2,1,0:T(8,128)(2,1)S(1)} %get-tuple-element.39), channel_id=1, source_target_pairs={{0,12},{4,8},{8,4},{12,0},{1,13},{5,9},{9,5},{13,1},{2,14},{6,10},... | collective-permute-start | bytes 393224 | tf_op jit(solution)/shard_map/ppermute | solution.py:218
  20.0 15.2 %collective-permute-done.5.refs_3_ = bf16[2,64,1024]{2,1,0:T(8,128)(2,1)S(1)} collective-permute-done((bf16[2,64,1024]{2,1,0:T(8,128)(2,1)S(1)}, bf16[2,64,1024]{2,1,0:T(8,128)(2,1)S(1)}, u32[]{:S(2)}, u32[]{:S(2)}) %collective-permute-start.5) | collective-permute-done | bytes 262176 | tf_op jit(solution)/shard_map/ppermute | solution.py:218
  35.2 0.0 copy-done
  35.2 0.0 copy-done.2
  35.2 2.1 %middle.2 = (bf16[2,64,1024]{2,1,0:T(8,128)(2,1)S(1)}, bf16[2,64,1024]{2,1,0:T(8,128)(2,1)S(1)}, bf16[2,64,1024]{2,1,0:T(8,128)(2,1)S(1)}, bf16[2,64,1024]{2,1,0:T(8,128)(2,1)S(1)}, f32[2,256,256]{2,1,0:T(8,128)S(1)}) custom-call(bf16[2,256,256]{2,1,0:T(8,128)(2,1)S(1)} %copy-done.2, bf16[1536,512]{1,0:T(8,128)(2,1)S(1)} %copy-done, ...), custom_call_target="tpu_custom_call" | custom-call | tf_op jit(solution)/shard_map/middle/pallas_call | solution.py:131
  37.3 0.0 collective-permute-done.refs_1_
  37.3 0.0 collective-permute-done.1.refs_2_
  37.3 4.6 %collective-permute-done.2.refs_3_ = bf16[2,64,512]{2,1,0:T(8,128)(2,1)S(1)} collective-permute-done((bf16[2,64,512]{2,1,0:T(8,128)(2,1)S(1)}, bf16[2,64,512]{2,1,0:T(8,128)(2,1)S(1)}, u32[]{:S(2)}, u32[]{:S(2)}) %collective-permute-start.2) | collective-permute-done | bytes 131104 | tf_op jit(solution)/shard_map/ppermute | solution.py:218
  41.9 1.0 middle.3
  42.9 0.0 collective-permute-done.10
  42.9 1.7 %pad_maximum_fusion.1 = bf16[2,1536,512]{2,1,0:T(8,128)(2,1)S(1)} fusion(bf16[1,1536,512]{2,1,0:T(8,128)(2,1)S(1)} %collective-permute-done.10, bf16[1,1536,512]{2,1,0:T(8,128)(2,1)} %bitcast), kind=kLoop, calls=%fused_computation.1 | loop fusion | flops 1572864 | bytes 6291456 | tf_op jit(solution)/shard_map/concatenate | solution.py:238
  44.6 2.5 %collective-permute-start.11 = (bf16[2,1536,512]{2,1,0:T(8,128)(2,1)S(1)}, bf16[2,1536,512]{2,1,0:T(8,128)(2,1)S(1)}, u32[]{:S(2)}, u32[]{:S(2)}) collective-permute-start(bf16[2,1536,512]{2,1,0:T(8,128)(2,1)S(1)} %pad_maximum_fusion.1), channel_id=1, source_target_pairs={{0,1},{1,0},{2,3},{3,2},{4,5},{5,4},{6,7},{7,6},{8,9},{9,8},{10,11... | collective-permute-start | bytes 9437192 | tf_op jit(solution)/shard_map/ppermute | solution.py:241
  47.1 1.9 %collective-permute-start.12 = (bf16[2,64,1024]{2,1,0:T(8,128)(2,1)S(1)}, bf16[2,64,1024]{2,1,0:T(8,128)(2,1)S(1)}, u32[]{:S(2)}, u32[]{:S(2)}) collective-permute-start(bf16[2,64,1024]{2,1,0:T(8,128)(2,1)S(1)} %get-tuple-element.52), channel_id=1, source_target_pairs={{0,0},{1,4},{2,8},{3,12},{4,1},{5,5},{6,9},{7,13},{8,2},{9,6},{10,... | collective-permute-start | bytes 786440 | tf_op jit(solution)/shard_map/ppermute | solution.py:236
  49.0 14.1 %collective-permute-done.12.refs_0_ = bf16[2,64,1024]{2,1,0:T(8,128)(2,1)S(1)} collective-permute-done((bf16[2,64,1024]{2,1,0:T(8,128)(2,1)S(1)}, bf16[2,64,1024]{2,1,0:T(8,128)(2,1)S(1)}, u32[]{:S(2)}, u32[]{:S(2)}) %collective-permute-start.12) | collective-permute-done | bytes 262176 | tf_op jit(solution)/shard_map/ppermute | solution.py:236
  63.0 0.0 collective-permute-start.16
  63.0 0.0 collective-permute-start.17
  63.0 2.1 %collective-permute-start.18 = (f32[2,64,256]{2,1,0:T(8,128)S(1)}, f32[2,64,256]{2,1,0:T(8,128)S(1)}, u32[]{:S(2)}, u32[]{:S(2)}) collective-permute-start(f32[2,64,256]{2,1,0:T(8,128)S(1)} %get-tuple-element.59), channel_id=1, source_target_pairs={{0,3},{1,2},{2,1},{3,0},{4,7},{5,6},{6,5},{7,4},{8,11},{9,10},{10,... | collective-permute-start | bytes 393224 | tf_op jit(solution)/shard_map/ppermute | solution.py:246
  65.2 1.7 %collective-permute-start.13 = (bf16[2,64,1024]{2,1,0:T(8,128)(2,1)S(1)}, bf16[2,64,1024]{2,1,0:T(8,128)(2,1)S(1)}, u32[]{:S(2)}, u32[]{:S(2)}) collective-permute-start(bf16[2,64,1024]{2,1,0:T(8,128)(2,1)S(1)} %get-tuple-element.53), channel_id=1, source_target_pairs={{0,4},{1,0},{2,12},{3,8},{4,5},{5,1},{6,13},{7,9},{8,6},{9,2},{10,... | collective-permute-start | bytes 786440 | tf_op jit(solution)/shard_map/ppermute | solution.py:236
  66.8 0.0 collective-permute-done.16
  66.8 0.0 collective-permute-start.14
  66.8 0.7 collective-permute-done.17
  67.6 2.7 %collective-permute-start.15 = (bf16[2,64,1024]{2,1,0:T(8,128)(2,1)S(1)}, bf16[2,64,1024]{2,1,0:T(8,128)(2,1)S(1)}, u32[]{:S(2)}, u32[]{:S(2)}) collective-permute-start(bf16[2,64,1024]{2,1,0:T(8,128)(2,1)S(1)} %get-tuple-element.55), channel_id=1, source_target_pairs={{0,12},{1,8},{2,4},{3,0},{4,13},{5,9},{6,5},{7,1},{8,14},{9,10},{1... | collective-permute-start | bytes 786440 | tf_op jit(solution)/shard_map/ppermute | solution.py:236
  70.3 4.5 %collective-permute-done.18 = f32[2,64,256]{2,1,0:T(8,128)S(1)} collective-permute-done((f32[2,64,256]{2,1,0:T(8,128)S(1)}, f32[2,64,256]{2,1,0:T(8,128)S(1)}, u32[]{:S(2)}, u32[]{:S(2)}) %collective-permute-start.18) | collective-permute-done | bytes 131104 | tf_op jit(solution)/shard_map/ppermute | solution.py:246
  74.8 2.3 %collective-permute-start.6 = (bf16[2,64,512]{2,1,0:T(8,128)(2,1)S(1)}, bf16[2,64,512]{2,1,0:T(8,128)(2,1)S(1)}, u32[]{:S(2)}, u32[]{:S(2)}) collective-permute-start(bf16[2,64,512]{2,1,0:T(8,128)(2,1)S(1)} %get-tuple-element.41), channel_id=1, source_target_pairs={{0,0},{1,4},{2,8},{3,12},{4,1},{5,5},{6,9},{7,13},{8,2},{9,6},{10,... | collective-permute-start | bytes 393224 | tf_op jit(solution)/shard_map/ppermute | solution.py:236
  77.0 0.7 add_multiply_fusion
  77.7 0.0 collective-permute-done.11
  77.7 1.7 %collective-permute-start.7 = (bf16[2,64,512]{2,1,0:T(8,128)(2,1)S(1)}, bf16[2,64,512]{2,1,0:T(8,128)(2,1)S(1)}, u32[]{:S(2)}, u32[]{:S(2)}) collective-permute-start(bf16[2,64,512]{2,1,0:T(8,128)(2,1)S(1)} %get-tuple-element.42), channel_id=1, source_target_pairs={{0,4},{1,0},{2,12},{3,8},{4,5},{5,1},{6,13},{7,9},{8,6},{9,2},{10,... | collective-permute-start | bytes 393224 | tf_op jit(solution)/shard_map/ppermute | solution.py:236
  79.4 0.1 collective-permute-done.13.refs_1_
  79.5 0.0 collective-permute-start.8
  79.5 12.5 %collective-permute-done.14.refs_2_ = bf16[2,64,1024]{2,1,0:T(8,128)(2,1)S(1)} collective-permute-done((bf16[2,64,1024]{2,1,0:T(8,128)(2,1)S(1)}, bf16[2,64,1024]{2,1,0:T(8,128)(2,1)S(1)}, u32[]{:S(2)}, u32[]{:S(2)}) %collective-permute-start.14) | collective-permute-done | bytes 262176 | tf_op jit(solution)/shard_map/ppermute | solution.py:236
  92.1 0.2 collective-permute-start.9
  92.3 4.2 %pad_maximum_fusion.refs_4_ = bf16[4,1536,512]{2,1,0:T(8,128)(2,1)} fusion(bf16[2,1536,512]{2,1,0:T(8,128)(2,1)S(1)} %collective-permute-done.11, bf16[1,1536,512]{2,1,0:T(8,128)(2,1)S(1)} %collective-permute-done.10, bf16[1,1536,512]{2,1,0:T(8,128)(2,1)} %bitcast), kind=kLoop, calls=%fused_computation | loop fusion | flops 6291456 | bytes 12582912 | tf_op jit(solution)/shard_map/concatenate | solution.py:238
  96.5 1.6 %collective-permute-done.15.refs_3_ = bf16[2,64,1024]{2,1,0:T(8,128)(2,1)S(1)} collective-permute-done((bf16[2,64,1024]{2,1,0:T(8,128)(2,1)S(1)}, bf16[2,64,1024]{2,1,0:T(8,128)(2,1)S(1)}, u32[]{:S(2)}, u32[]{:S(2)}) %collective-permute-start.15) | collective-permute-done | bytes 262176 | tf_op jit(solution)/shard_map/ppermute | solution.py:236
  98.1 3.0 %left_rows.2.refs_5_ = f32[2,64,256]{2,1,0:T(8,128)S(1)} custom-call(bf16[2,64,1024]{2,1,0:T(8,128)(2,1)S(1)} %collective-permute-done.12.refs_0_, bf16[2,64,1024]{2,1,0:T(8,128)(2,1)S(1)} %collective-permute-done.13.refs_1_, bf16[2,64,1024]{2,1,0:T(8,128)(2,1)S(1)} %collective-permute-done.14.refs_2_, ...), custom_call_target="tpu_custom_call" | custom-call | tf_op jit(solution)/shard_map/left_rows/pallas_call | solution.py:179
  101.2 0.0 collective-permute-done.6.refs_0_
  101.2 0.0 collective-permute-done.7.refs_1_
  101.2 0.0 collective-permute-done.8.refs_2_
  101.2 2.3 %collective-permute-done.9.refs_3_ = bf16[2,64,512]{2,1,0:T(8,128)(2,1)S(1)} collective-permute-done((bf16[2,64,512]{2,1,0:T(8,128)(2,1)S(1)}, bf16[2,64,512]{2,1,0:T(8,128)(2,1)S(1)}, u32[]{:S(2)}, u32[]{:S(2)}) %collective-permute-start.9) | collective-permute-done | bytes 131104 | tf_op jit(solution)/shard_map/ppermute | solution.py:236
  103.5 2.7 %left_rows.3 = f32[2,64,256]{2,1,0:T(8,128)} custom-call(bf16[2,64,512]{2,1,0:T(8,128)(2,1)S(1)} %collective-permute-done.6.refs_0_, bf16[2,64,512]{2,1,0:T(8,128)(2,1)S(1)} %collective-permute-done.7.refs_1_, bf16[2,64,512]{2,1,0:T(8,128)(2,1)S(1)} %collective-permute-done.8.refs_2_, bf16[2,64,512]{2,1,0:T(8,128)(2,1)S(1)} %collective-permute-done.9.refs_3_, ...), custom_call_target="tpu_custom_call" | custom-call | tf_op jit(solution)/shard_map/left_rows/pallas_call | solution.py:179
Async XLA Ops:
  0.6 1.0 copy-start.1
  1.6 33.6 %copy-start = (bf16[1536,512]{1,0:T(8,128)(2,1)S(1)}, bf16[1536,512]{1,0:T(8,128)(2,1)}, u32[]{:S(2)}) copy-start(bf16[1536,512]{1,0:T(8,128)(2,1)} %targets_ref.3) | copy-start | bytes 4718596
  1.6 33.6 %copy-start.2 = (bf16[2,256,256]{2,1,0:T(8,128)(2,1)S(1)}, bf16[2,256,256]{2,1,0:T(8,128)(2,1)}, u32[]{:S(2)}) copy-start(bf16[2,256,256]{2,1,0:T(8,128)(2,1)} %right_ref.3) | copy-start | bytes 786436
  4.9 37.9 %collective-permute-start.10 = (bf16[1,1536,512]{2,1,0:T(8,128)(2,1)}, bf16[1,1536,512]{2,1,0:T(8,128)(2,1)S(1)}, u32[]{:S(2)}, u32[]{:S(2)}) collective-permute-start(bf16[1,1536,512]{2,1,0:T(8,128)(2,1)} %bitcast), channel_id=1, source_target_pairs={{0,2},{1,3},{2,0},{3,1},{4,6},{5,7},{6,4},{7,5},{8,10},{9,11},{10,... | collective-permute-start | bytes 4718600 | tf_op jit(solution)/shard_map/ppermute | solution.py:223
  6.2 10.3 %collective-permute-start.3 = (bf16[2,64,1024]{2,1,0:T(8,128)(2,1)S(1)}, bf16[2,64,1024]{2,1,0:T(8,128)(2,1)S(1)}, u32[]{:S(2)}, u32[]{:S(2)}) collective-permute-start(bf16[2,64,1024]{2,1,0:T(8,128)(2,1)S(1)} %get-tuple-element.32), channel_id=1, source_target_pairs={{0,4},{4,0},{8,12},{12,8},{1,5},{5,1},{9,13},{13,9},{2,6},{6,2},{1... | collective-permute-start | bytes 786440 | tf_op jit(solution)/shard_map/ppermute | solution.py:218
  7.5 11.1 %collective-permute-start.4 = (bf16[2,64,1024]{2,1,0:T(8,128)(2,1)S(1)}, bf16[2,64,1024]{2,1,0:T(8,128)(2,1)S(1)}, u32[]{:S(2)}, u32[]{:S(2)}) collective-permute-start(bf16[2,64,1024]{2,1,0:T(8,128)(2,1)S(1)} %get-tuple-element.33), channel_id=1, source_target_pairs={{0,8},{4,12},{8,0},{12,4},{1,9},{5,13},{9,1},{13,5},{2,10},{6,14},... | collective-permute-start | bytes 786440 | tf_op jit(solution)/shard_map/ppermute | solution.py:218
  7.6 27.6 %collective-permute-start.5 = (bf16[2,64,1024]{2,1,0:T(8,128)(2,1)S(1)}, bf16[2,64,1024]{2,1,0:T(8,128)(2,1)S(1)}, u32[]{:S(2)}, u32[]{:S(2)}) collective-permute-start(bf16[2,64,1024]{2,1,0:T(8,128)(2,1)S(1)} %get-tuple-element.34), channel_id=1, source_target_pairs={{0,12},{4,8},{8,4},{12,0},{1,13},{5,9},{9,5},{13,1},{2,14},{6,10},... | collective-permute-start | bytes 786440 | tf_op jit(solution)/shard_map/ppermute | solution.py:218
  8.9 28.4 %collective-permute-start = (bf16[2,64,512]{2,1,0:T(8,128)(2,1)S(1)}, bf16[2,64,512]{2,1,0:T(8,128)(2,1)S(1)}, u32[]{:S(2)}, u32[]{:S(2)}) collective-permute-start(bf16[2,64,512]{2,1,0:T(8,128)(2,1)S(1)} %get-tuple-element.37), channel_id=1, source_target_pairs={{0,4},{4,0},{8,12},{12,8},{1,5},{5,1},{9,13},{13,9},{2,6},{6,2},{1... | collective-permute-start | bytes 393224 | tf_op jit(solution)/shard_map/ppermute | solution.py:218
  16.6 20.7 %collective-permute-start.1 = (bf16[2,64,512]{2,1,0:T(8,128)(2,1)S(1)}, bf16[2,64,512]{2,1,0:T(8,128)(2,1)S(1)}, u32[]{:S(2)}, u32[]{:S(2)}) collective-permute-start(bf16[2,64,512]{2,1,0:T(8,128)(2,1)S(1)} %get-tuple-element.38), channel_id=1, source_target_pairs={{0,8},{4,12},{8,0},{12,4},{1,9},{5,13},{9,1},{13,5},{2,10},{6,14},... | collective-permute-start | bytes 393224 | tf_op jit(solution)/shard_map/ppermute | solution.py:218
  18.6 23.3 %collective-permute-start.2 = (bf16[2,64,512]{2,1,0:T(8,128)(2,1)S(1)}, bf16[2,64,512]{2,1,0:T(8,128)(2,1)S(1)}, u32[]{:S(2)}, u32[]{:S(2)}) collective-permute-start(bf16[2,64,512]{2,1,0:T(8,128)(2,1)S(1)} %get-tuple-element.39), channel_id=1, source_target_pairs={{0,12},{4,8},{8,4},{12,0},{1,13},{5,9},{9,5},{13,1},{2,14},{6,10},... | collective-permute-start | bytes 393224 | tf_op jit(solution)/shard_map/ppermute | solution.py:218
  44.6 33.2 %collective-permute-start.11 = (bf16[2,1536,512]{2,1,0:T(8,128)(2,1)S(1)}, bf16[2,1536,512]{2,1,0:T(8,128)(2,1)S(1)}, u32[]{:S(2)}, u32[]{:S(2)}) collective-permute-start(bf16[2,1536,512]{2,1,0:T(8,128)(2,1)S(1)} %pad_maximum_fusion.1), channel_id=1, source_target_pairs={{0,1},{1,0},{2,3},{3,2},{4,5},{5,4},{6,7},{7,6},{8,9},{9,8},{10,11... | collective-permute-start | bytes 9437192 | tf_op jit(solution)/shard_map/ppermute | solution.py:241
  47.1 16.0 %collective-permute-start.12 = (bf16[2,64,1024]{2,1,0:T(8,128)(2,1)S(1)}, bf16[2,64,1024]{2,1,0:T(8,128)(2,1)S(1)}, u32[]{:S(2)}, u32[]{:S(2)}) collective-permute-start(bf16[2,64,1024]{2,1,0:T(8,128)(2,1)S(1)} %get-tuple-element.52), channel_id=1, source_target_pairs={{0,0},{1,4},{2,8},{3,12},{4,1},{5,5},{6,9},{7,13},{8,2},{9,6},{10,... | collective-permute-start | bytes 786440 | tf_op jit(solution)/shard_map/ppermute | solution.py:236
  63.0 3.8 %collective-permute-start.16 = (f32[2,64,256]{2,1,0:T(8,128)S(1)}, f32[2,64,256]{2,1,0:T(8,128)S(1)}, u32[]{:S(2)}, u32[]{:S(2)}) collective-permute-start(f32[2,64,256]{2,1,0:T(8,128)S(1)} %get-tuple-element.57), channel_id=1, source_target_pairs={{0,1},{1,0},{2,3},{3,2},{4,5},{5,4},{6,7},{7,6},{8,9},{9,8},{10,11... | collective-permute-start | bytes 393224 | tf_op jit(solution)/shard_map/ppermute | solution.py:246
  63.0 4.6 %collective-permute-start.17 = (f32[2,64,256]{2,1,0:T(8,128)S(1)}, f32[2,64,256]{2,1,0:T(8,128)S(1)}, u32[]{:S(2)}, u32[]{:S(2)}) collective-permute-start(f32[2,64,256]{2,1,0:T(8,128)S(1)} %get-tuple-element.58), channel_id=1, source_target_pairs={{0,2},{1,3},{2,0},{3,1},{4,6},{5,7},{6,4},{7,5},{8,10},{9,11},{10,... | collective-permute-start | bytes 393224 | tf_op jit(solution)/shard_map/ppermute | solution.py:246
  63.0 11.7 %collective-permute-start.18 = (f32[2,64,256]{2,1,0:T(8,128)S(1)}, f32[2,64,256]{2,1,0:T(8,128)S(1)}, u32[]{:S(2)}, u32[]{:S(2)}) collective-permute-start(f32[2,64,256]{2,1,0:T(8,128)S(1)} %get-tuple-element.59), channel_id=1, source_target_pairs={{0,3},{1,2},{2,1},{3,0},{4,7},{5,6},{6,5},{7,4},{8,11},{9,10},{10,... | collective-permute-start | bytes 393224 | tf_op jit(solution)/shard_map/ppermute | solution.py:246
  65.2 14.4 %collective-permute-start.13 = (bf16[2,64,1024]{2,1,0:T(8,128)(2,1)S(1)}, bf16[2,64,1024]{2,1,0:T(8,128)(2,1)S(1)}, u32[]{:S(2)}, u32[]{:S(2)}) collective-permute-start(bf16[2,64,1024]{2,1,0:T(8,128)(2,1)S(1)} %get-tuple-element.53), channel_id=1, source_target_pairs={{0,4},{1,0},{2,12},{3,8},{4,5},{5,1},{6,13},{7,9},{8,6},{9,2},{10,... | collective-permute-start | bytes 786440 | tf_op jit(solution)/shard_map/ppermute | solution.py:236
  66.8 25.2 %collective-permute-start.14 = (bf16[2,64,1024]{2,1,0:T(8,128)(2,1)S(1)}, bf16[2,64,1024]{2,1,0:T(8,128)(2,1)S(1)}, u32[]{:S(2)}, u32[]{:S(2)}) collective-permute-start(bf16[2,64,1024]{2,1,0:T(8,128)(2,1)S(1)} %get-tuple-element.54), channel_id=1, source_target_pairs={{0,8},{1,12},{2,0},{3,4},{4,9},{5,13},{6,1},{7,5},{8,10},{9,14},{1... | collective-permute-start | bytes 786440 | tf_op jit(solution)/shard_map/ppermute | solution.py:236
  67.6 30.5 %collective-permute-start.15 = (bf16[2,64,1024]{2,1,0:T(8,128)(2,1)S(1)}, bf16[2,64,1024]{2,1,0:T(8,128)(2,1)S(1)}, u32[]{:S(2)}, u32[]{:S(2)}) collective-permute-start(bf16[2,64,1024]{2,1,0:T(8,128)(2,1)S(1)} %get-tuple-element.55), channel_id=1, source_target_pairs={{0,12},{1,8},{2,4},{3,0},{4,13},{5,9},{6,5},{7,1},{8,14},{9,10},{1... | collective-permute-start | bytes 786440 | tf_op jit(solution)/shard_map/ppermute | solution.py:236
  74.8 26.4 %collective-permute-start.6 = (bf16[2,64,512]{2,1,0:T(8,128)(2,1)S(1)}, bf16[2,64,512]{2,1,0:T(8,128)(2,1)S(1)}, u32[]{:S(2)}, u32[]{:S(2)}) collective-permute-start(bf16[2,64,512]{2,1,0:T(8,128)(2,1)S(1)} %get-tuple-element.41), channel_id=1, source_target_pairs={{0,0},{1,4},{2,8},{3,12},{4,1},{5,5},{6,9},{7,13},{8,2},{9,6},{10,... | collective-permute-start | bytes 393224 | tf_op jit(solution)/shard_map/ppermute | solution.py:236
  77.7 23.4 %collective-permute-start.7 = (bf16[2,64,512]{2,1,0:T(8,128)(2,1)S(1)}, bf16[2,64,512]{2,1,0:T(8,128)(2,1)S(1)}, u32[]{:S(2)}, u32[]{:S(2)}) collective-permute-start(bf16[2,64,512]{2,1,0:T(8,128)(2,1)S(1)} %get-tuple-element.42), channel_id=1, source_target_pairs={{0,4},{1,0},{2,12},{3,8},{4,5},{5,1},{6,13},{7,9},{8,6},{9,2},{10,... | collective-permute-start | bytes 393224 | tf_op jit(solution)/shard_map/ppermute | solution.py:236
  79.5 21.6 %collective-permute-start.8 = (bf16[2,64,512]{2,1,0:T(8,128)(2,1)S(1)}, bf16[2,64,512]{2,1,0:T(8,128)(2,1)S(1)}, u32[]{:S(2)}, u32[]{:S(2)}) collective-permute-start(bf16[2,64,512]{2,1,0:T(8,128)(2,1)S(1)} %get-tuple-element.43), channel_id=1, source_target_pairs={{0,8},{1,12},{2,0},{3,4},{4,9},{5,13},{6,1},{7,5},{8,10},{9,14},{1... | collective-permute-start | bytes 393224 | tf_op jit(solution)/shard_map/ppermute | solution.py:236
  92.1 11.4 %collective-permute-start.9 = (bf16[2,64,512]{2,1,0:T(8,128)(2,1)S(1)}, bf16[2,64,512]{2,1,0:T(8,128)(2,1)S(1)}, u32[]{:S(2)}, u32[]{:S(2)}) collective-permute-start(bf16[2,64,512]{2,1,0:T(8,128)(2,1)S(1)} %get-tuple-element.44), channel_id=1, source_target_pairs={{0,12},{1,8},{2,4},{3,0},{4,13},{5,9},{6,5},{7,1},{8,14},{9,10},{1... | collective-permute-start | bytes 393224 | tf_op jit(solution)/shard_map/ppermute | solution.py:236

commit v2 on v0

v2 whole, which is shorter than its diff:
```python
import functools

import jax
import jax.numpy as jnp
from jax import lax
from jax.experimental import pallas as pl
from jax.experimental.pallas import tpu as pltpu
from jax.sharding import PartitionSpec as P

F32, BF16 = jnp.float32, jnp.bfloat16
NT = (((1,), (1,)), ((), ()))
NN = (((1,), (0,)), ((), ()))
TN = (((0,), (0,)), ((), ()))


def dot(a, b, dims):
    return lax.dot_general(a, b, dims, preferred_element_type=F32)


def after(value, *others):
    return lax.optimization_barrier((value, others))[0]


def call(kernel, name, flops, **kwargs):
    moved = sum(
        s.size * s.dtype.itemsize for s in jax.tree.leaves(kwargs["out_shape"])
    )
    return pl.pallas_call(
        kernel,
        name=name,
        compiler_params=pltpu.CompilerParams(vmem_limit_bytes=24 << 20),
        cost_estimate=pl.CostEstimate(flops=flops, bytes_accessed=2 * moved, transcendentals=0),
        **kwargs,
    )


def whole(shape):
    return pl.BlockSpec(shape, lambda i: (0,) * len(shape))


def forward_kernel(peers, g, left_ref, x_ref, *refs):
    outs, held = refs[:peers], refs[peers]
    blocks, width = left_ref.shape[0], left_ref.shape[1]
    rows = width // peers
    step = rows // blocks
    me = lax.axis_index("blk")

    @pl.when(pl.program_id(0) == 0)
    def _():
        for d in range(peers):
            at = pl.multiple_of((me ^ d) * rows + g * step, step)
            for k in range(blocks):
                held[k, d * step : (d + 1) * step, :] = left_ref[k, pl.ds(at, step), :]

    for k in range(blocks):
        first = dot(held[k], x_ref[:, k * width : (k + 1) * width], NT).astype(BF16)
        for d in range(peers):
            outs[d][k] = first[d * step : (d + 1) * step]


def forward(left, x, peers, g, tile):
    blocks, width, _ = left.shape
    step = width // peers // blocks
    tokens = x.shape[0]
    return call(
        functools.partial(forward_kernel, peers, g),
        "forward",
        2 * tokens * width * width,
        grid=(tokens // tile,),
        in_specs=[whole(left.shape), pl.BlockSpec((tile, x.shape[1]), lambda i: (i, 0))],
        out_specs=[pl.BlockSpec((blocks, step, tile), lambda i: (0, 0, i))] * peers,
        out_shape=[jax.ShapeDtypeStruct((blocks, step, tokens), BF16)] * peers,
        scratch_shapes=[pltpu.VMEM((blocks, peers * step, width), BF16)],
    )(left, x)


def middle_kernel(peers, toks, g, right_ref, targets_ref, *refs):
    pieces, backs, terms = refs[:peers], refs[peers : 2 * peers], refs[2 * peers : 2 * peers + toks]
    mixed, back, total = refs[2 * peers + toks :]
    blocks, step, _ = pieces[0].shape
    width = right_ref.shape[1]
    rows = blocks * step
    me, own = lax.axis_index("blk"), lax.axis_index("tok")
    i = pl.program_id(0)

    @pl.when(i == 0)
    def _():
        total[...] = jnp.zeros_like(total)

    for d in range(peers):
        for k in range(blocks):
            at = pl.multiple_of((me ^ d) * rows + k * step, step)
            mixed[pl.ds(at, step), :] = pieces[d][k]
    error = (dot(right_ref[g], mixed[...], NN) - targets_ref[...].astype(F32).T).astype(BF16)
    back[...] = dot(right_ref[g], error, TN).astype(BF16)
    for d in range(peers):
        for k in range(blocks):
            at = pl.multiple_of((me ^ d) * rows + k * step, step)
            backs[d][k] = back[pl.ds(at, step), :]
    total[...] += dot(error, mixed[...], NT)

    @pl.when(i == pl.num_programs(0) - 1)
    def _():
        size = width // toks
        for s in range(toks):
            at = pl.multiple_of((own ^ s) * size, size)
            terms[s][...] = total[pl.ds(at, size), :]


def middle(right, targets, pieces, toks, g, tile):
    peers = len(pieces)
    blocks, step, tokens = pieces[0].shape
    width = right.shape[1]
    piece = pl.BlockSpec((blocks, step, tile), lambda i: (0, 0, i))
    term = (width // toks, width)
    return call(
        functools.partial(middle_kernel, peers, toks, g),
        "middle",
        6 * tokens * width * width,
        grid=(tokens // tile,),
        in_specs=[whole(right.shape), pl.BlockSpec((tile, width), lambda i: (i, g))]
        + [piece] * peers,
        out_specs=[piece] * peers + [whole(term)] * toks,
        out_shape=[jax.ShapeDtypeStruct(pieces[0].shape, BF16)] * peers
        + [jax.ShapeDtypeStruct(term, F32)] * toks,
        scratch_shapes=[
            pltpu.VMEM((width, tile), BF16),
            pltpu.VMEM((width, tile), BF16),
            pltpu.VMEM((width, width), F32),
        ],
    )(right, targets, *pieces)


def left_kernel(peers, toks, carried, x_ref, *refs):
    pieces, refs = refs[:peers], refs[peers:]
    extras, outs, (joined, partial) = refs[: carried * toks], refs[carried * toks : -2], refs[-2:]
    blocks, step, _ = pieces[0].shape
    width = x_ref.shape[1] // blocks
    mine = lax.axis_index("blk") ^ lax.axis_index("tok")
    for k in range(blocks):
        for d in range(peers):
            joined[d * step : (d + 1) * step, :] = pieces[d][k]
        partial[k] = dot(joined[...], x_ref[:, k * width : (k + 1) * width], NN)
    for s in range(toks):
        at = pl.multiple_of((mine ^ s) * step, step)
        for k in range(blocks):
            outs[s][carried, k * step : (k + 1) * step, :] = partial[k, pl.ds(at, step), :]
        for n in range(carried):
            outs[s][n] = extras[n * toks + s][...]


def left_terms(x, pieces, extras, toks):
    peers = len(pieces)
    blocks, step, tokens = pieces[0].shape
    width = x.shape[1] // blocks
    carried = len(extras)
    flat = [e[s] for e in extras for s in range(toks)]
    return call(
        functools.partial(left_kernel, peers, toks, carried),
        "left_terms",
        2 * tokens * width * width,
        in_specs=[pl.BlockSpec(memory_space=pltpu.VMEM)] * (1 + peers + len(flat)),
        out_specs=[pl.BlockSpec(memory_space=pltpu.VMEM)] * toks,
        out_shape=[jax.ShapeDtypeStruct((carried + 1, blocks * step, width), F32)] * toks,
        scratch_shapes=[
            pltpu.VMEM((peers * step, tokens), BF16),
            pltpu.VMEM((blocks, peers * step, width), F32),
        ],
    )(x, *pieces, *flat)


def finish_kernel(toks, groups, scale, *refs):
    sums = refs[: toks * groups]
    left_out, right_out = refs[toks * groups :]
    blocks, rows, _ = left_out.shape
    step = rows // groups
    for g in range(groups):
        parts = sums[g * toks : (g + 1) * toks]
        last = parts[0].shape[0] - 1
        total = parts[0][last]
        for p in parts[1:]:
            total = total + p[last]
        total = total * scale
        for k in range(blocks):
            left_out[k, g * step : (g + 1) * step, :] = total[k * step : (k + 1) * step]
        if last:
            for n in range(last):
                total = parts[0][n]
                for p in parts[1:]:
                    total = total + p[n]
                right_out[n] = total * scale


def finish(groups, blocks, scale):
    toks = len(groups[0])
    _, rows, width = groups[0][0].shape
    flat = [a for group in groups for a in group]
    shape = jax.ShapeDtypeStruct((blocks, rows, width), F32)
    return call(
        functools.partial(finish_kernel, toks, len(groups), scale),
        "finish",
        1,
        in_specs=[pl.BlockSpec(memory_space=pltpu.VMEM)] * len(flat),
        out_specs=[pl.BlockSpec(memory_space=pltpu.VMEM)] * 2,
        out_shape=[shape] * 2,
    )(*flat)


def on_device(inputs, targets, left_factor, right_factor):
    tokens = inputs.shape[0]
    blocks = left_factor.shape[0]
    peers = lax.axis_size("blk")
    toks = lax.axis_size("tok")
    tile = tokens // 3

    def swap(axis, size, d, value):
        return lax.ppermute(value, axis, [(j, j ^ d) for j in range(size)])

    def exchange(axis, pieces):
        size = len(pieces)
        got = {d: swap(axis, size, d, pieces[d]) for d in range(size - 1, 0, -1)}
        return [pieces[0]] + [got[d] for d in range(1, size)]

    left, arrived = left_factor, []
    for g in range(blocks):
        sent = forward(left, inputs, peers, g, tile)
        left = after(left_factor, *sent)
        arrived.append(exchange("blk", sent))

    right, returned, terms = right_factor, [], []
    for g in range(blocks):
        res = middle(right, targets, arrived[g], toks, g, tile)
        right = after(right_factor, *res[:peers])
        returned.append(exchange("blk", res[:peers]))
        terms.append(res[peers:])

    rows, sums = inputs, []
    for g in range(blocks):
        out = left_terms(rows, returned[g], terms if g == 0 else [], toks)
        rows = after(inputs, *out)
        sums.append(exchange("tok", out))
    return tuple(finish(sums, blocks, 1.0 / tokens))


def solution(mesh):
    in_specs = (
        P(("groups", "tok"), "blk"),
        P(("groups", "tok"), "blk"),
        P(("groups", "blk"), None, None),
        P(("groups", "blk"), None, None),
    )
    out_specs = (P(("groups", "blk"), "tok", None), P(("groups", "blk"), "tok", None))
    return jax.shard_map(
        on_device, mesh=mesh, in_specs=in_specs, out_specs=out_specs, check_vma=False
    )
```

time: 134 us -> 84.1 us (0.63); the launches traced: 132 us -> 83.8 us
  waiting for transfers between devices: 80.3 us -> 53.3 us
  between operations: 14.1 us -> 0.73 us
  local copies, waits for them, and re-layouts: 14 us -> 2.37 us
  matrix products: 8.53 us -> 0 us
  starting transfers between devices: 11.3 us -> 19.6 us
  Pallas kernels: 0 us -> 7.77 us
  other arithmetic: 3.34 us -> 0 us
    all_to_all x2 -> x0, waiting for transfers between devices: 57.4 us -> none  [the longest x1 28.9 us: on_device(): lax.all_to_all(outgoing, 'blk', split_axis=1, concat_axis=0, tiled=True)]
    ppermute x0 -> x18, waiting for transfers between devices: none -> 53.3 us  [swap(): return lax.ppermute(value, axis, [(j, j ^ d) for j in range(size)])]
    reduce_scatter x2 -> x0, waiting for transfers between devices: 22.9 us -> none  [the longest x1 22.8 us: on_device(): lax.psum_scatter(term_left, 'tok', scatter_dimension=1, tiled=True)]
    ppermute x0 -> x18, starting transfers between devices: none -> 19.6 us  [swap(): return lax.ppermute(value, axis, [(j, j ^ d) for j in range(size)])]
    all_to_all x2 -> x0, starting transfers between devices: 11.3 us -> none  [the longest x1 6.53 us: on_device(): lax.all_to_all(backward_in, 'blk', split_axis=0, concat_axis=1, tiled=True)]
    dot_general x4 -> x0, matrix products: 7.91 us -> none  [the longest x1 2.78 us: on_device(): jnp.einsum('got,kgmt->gokm', error_rows, mixed_part, preferred_element_ty...]
    pallas_call x0 -> x7, Pallas kernels: none -> 7.77 us  [the longest x2 4.18 us: middle(): call(functools.partial(middle_kernel, peers, toks, g), 'middle', 6 * toke...]
    unnamed x14 -> x10, local copies, waits for them, and re-layouts: 7.16 us -> 2.37 us
  transfers between devices with their start and end apart: 4 -> 18, of which waited for: 3 -> 10; matrix products, arithmetic and copies ran while one was open for 9% -> 0% of each run, Pallas kernels for 0% -> 7%
where the time goes in v2:
time: 84.1 us; the launch traced here: 83.8 us
  waiting for transfers between devices  53.3 us (63%)
  starting transfers between devices  19.6 us (23%)
  Pallas kernels  7.77 us (9%)
  local copies, waits for them, and re-layouts  2.37 us (3%)
    ppermute x18, waiting for transfers between devices, swap(): return lax.ppermute(value, axis, [(j, j ^ d) for j in range(size)])  53.3 us
    ppermute x18, starting transfers between devices, swap(): return lax.ppermute(value, axis, [(j, j ^ d) for j in range(size)])  19.6 us
    pallas_call x2, Pallas kernels, middle(): call(functools.partial(middle_kernel, peers, toks, g), 'middle', 6 * toke...  4.18 us
    unnamed x10, local copies, waits for them, and re-layouts  2.37 us
    pallas_call x2, Pallas kernels, forward(): call(functools.partial(forward_kernel, peers, g), 'forward', 2 * tokens *...  2.04 us
  transfers between devices with their start and end apart: 18, of which 10 were waited for; matrix products, arithmetic and copies ran while one was open for 0% of the time, Pallas kernels for 7%

profile of v2, /device:TPU:21, one launch (start us, length us, event | category | flops | bytes accessed | tf_op | source)
XLA Modules:
  0.0 83.8 jit_solution(6246895423533157288)
XLA Ops:
  0.6 0.0 copy-start
  0.6 1.4 %copy-done = bf16[1536,512]{1,0:T(8,128)(2,1)S(1)} copy-done((bf16[1536,512]{1,0:T(8,128)(2,1)S(1)}, bf16[1536,512]{1,0:T(8,128)(2,1)}, u32[]{:S(2)}) %copy-start) | copy-done | bytes 1572888
  2.0 0.0 copy-start.3
  2.0 0.9 %copy-done.3 = bf16[2,256,256]{2,1,0:T(8,128)(2,1)S(1)} copy-done((bf16[2,256,256]{2,1,0:T(8,128)(2,1)S(1)}, bf16[2,256,256]{2,1,0:T(8,128)(2,1)}, u32[]{:S(2)}) %copy-start.3) | copy-done | bytes 262168
  3.0 0.0 copy-start.2
  3.0 0.0 copy-start.4
  3.0 1.0 %forward.2 = (bf16[2,32,1536]{2,1,0:T(8,128)(2,1)S(1)}, bf16[2,32,1536]{2,1,0:T(8,128)(2,1)S(1)}, bf16[2,32,1536]{2,1,0:T(8,128)(2,1)S(1)}, bf16[2,32,1536]{2,1,0:T(8,128)(2,1)S(1)}) custom-call(bf16[2,256,256]{2,1,0:T(8,128)(2,1)S(1)} %copy-done.3, bf16[1536,512]{1,0:T(8,128)(2,1)S(1)} %copy-done), custom_call_target="tpu_custom_call" | custom-call | flops 201326592 | bytes 1572864 | tf_op jit(solution)/shard_map/forward/pallas_call | solution.py:65
  4.0 1.4 %collective-permute-start = (bf16[2,32,1536]{2,1,0:T(8,128)(2,1)S(1)}, bf16[2,32,1536]{2,1,0:T(8,128)(2,1)S(1)}, u32[]{:S(2)}, u32[]{:S(2)}) collective-permute-start(bf16[2,32,1536]{2,1,0:T(8,128)(2,1)S(1)} %get-tuple-element.38), channel_id=1, source_target_pairs={{0,4},{4,0},{8,12},{12,8},{1,5},{5,1},{9,13},{13,9},{2,6},{6,2},{1... | collective-permute-start | bytes 589832 | tf_op jit(solution)/shard_map/ppermute | solution.py:217
  5.4 0.1 collective-permute-start.1
  5.4 1.3 %collective-permute-start.2 = (bf16[2,32,1536]{2,1,0:T(8,128)(2,1)S(1)}, bf16[2,32,1536]{2,1,0:T(8,128)(2,1)S(1)}, u32[]{:S(2)}, u32[]{:S(2)}) collective-permute-start(bf16[2,32,1536]{2,1,0:T(8,128)(2,1)S(1)} %get-tuple-element.40), channel_id=1, source_target_pairs={{0,12},{4,8},{8,4},{12,0},{1,13},{5,9},{9,5},{13,1},{2,14},{6,10},... | collective-permute-start | bytes 589832 | tf_op jit(solution)/shard_map/ppermute | solution.py:217
  6.7 1.0 %forward.3 = (bf16[2,32,1536]{2,1,0:T(8,128)(2,1)S(1)}, bf16[2,32,1536]{2,1,0:T(8,128)(2,1)S(1)}, bf16[2,32,1536]{2,1,0:T(8,128)(2,1)S(1)}, bf16[2,32,1536]{2,1,0:T(8,128)(2,1)S(1)}) custom-call(bf16[2,256,256]{2,1,0:T(8,128)(2,1)S(1)} %copy-done.3, bf16[1536,512]{1,0:T(8,128)(2,1)S(1)} %copy-done), custom_call_target="tpu_custom_call" | custom-call | flops 201326592 | bytes 1572864 | tf_op jit(solution)/shard_map/forward/pallas_call | solution.py:65
  7.8 2.3 %collective-permute-start.6 = (bf16[2,32,1536]{2,1,0:T(8,128)(2,1)S(1)}, bf16[2,32,1536]{2,1,0:T(8,128)(2,1)S(1)}, u32[]{:S(2)}, u32[]{:S(2)}) collective-permute-start(bf16[2,32,1536]{2,1,0:T(8,128)(2,1)S(1)} %get-tuple-element.52), channel_id=1, source_target_pairs={{0,4},{4,0},{8,12},{12,8},{1,5},{5,1},{9,13},{13,9},{2,6},{6,2},{1... | collective-permute-start | bytes 589832 | tf_op jit(solution)/shard_map/ppermute | solution.py:217
  10.0 0.0 collective-permute-start.7
  10.0 1.7 %collective-permute-done.refs_1_ = bf16[2,32,1536]{2,1,0:T(8,128)(2,1)S(1)} collective-permute-done((bf16[2,32,1536]{2,1,0:T(8,128)(2,1)S(1)}, bf16[2,32,1536]{2,1,0:T(8,128)(2,1)S(1)}, u32[]{:S(2)}, u32[]{:S(2)}) %collective-permute-start) | collective-permute-done | bytes 196640 | tf_op jit(solution)/shard_map/ppermute | solution.py:217
  11.7 0.0 collective-permute-start.8
  11.7 2.3 %collective-permute-done.1.refs_2_ = bf16[2,32,1536]{2,1,0:T(8,128)(2,1)S(1)} collective-permute-done((bf16[2,32,1536]{2,1,0:T(8,128)(2,1)S(1)}, bf16[2,32,1536]{2,1,0:T(8,128)(2,1)S(1)}, u32[]{:S(2)}, u32[]{:S(2)}) %collective-permute-start.1) | collective-permute-done | bytes 196640 | tf_op jit(solution)/shard_map/ppermute | solution.py:217
  14.0 10.6 %collective-permute-done.2.refs_3_ = bf16[2,32,1536]{2,1,0:T(8,128)(2,1)S(1)} collective-permute-done((bf16[2,32,1536]{2,1,0:T(8,128)(2,1)S(1)}, bf16[2,32,1536]{2,1,0:T(8,128)(2,1)S(1)}, u32[]{:S(2)}, u32[]{:S(2)}) %collective-permute-start.2) | collective-permute-done | bytes 196640 | tf_op jit(solution)/shard_map/ppermute | solution.py:217
  24.5 0.0 copy-done.2
  24.6 0.0 copy-done.4
  24.6 2.1 %middle.2 = (bf16[2,32,1536]{2,1,0:T(8,128)(2,1)S(1)}, bf16[2,32,1536]{2,1,0:T(8,128)(2,1)S(1)}, bf16[2,32,1536]{2,1,0:T(8,128)(2,1)S(1)}, bf16[2,32,1536]{2,1,0...) custom-call(bf16[2,256,256]{2,1,0:T(8,128)(2,1)S(1)} %copy-done.4, ...), custom_call_target="tpu_custom_call" | custom-call | flops 603979776 | bytes 2097152 | tf_op jit(solution)/shard_map/middle/pallas_call | solution.py:116
  26.7 0.0 copy-start.1
  26.7 0.1 collective-permute-start.3
  26.7 0.3 collective-permute-start.4
  27.0 0.0 collective-permute-done.6.refs_1_
  27.0 2.4 %collective-permute-start.5 = (bf16[2,32,1536]{2,1,0:T(8,128)(2,1)S(1)}, bf16[2,32,1536]{2,1,0:T(8,128)(2,1)S(1)}, u32[]{:S(2)}, u32[]{:S(2)}) collective-permute-start(bf16[2,32,1536]{2,1,0:T(8,128)(2,1)S(1)} %get-tuple-element.44), channel_id=1, source_target_pairs={{0,12},{4,8},{8,4},{12,0},{1,13},{5,9},{9,5},{13,1},{2,14},{6,10},... | collective-permute-start | bytes 589832 | tf_op jit(solution)/shard_map/ppermute | solution.py:217
  29.4 8.8 %collective-permute-done.7.refs_2_ = bf16[2,32,1536]{2,1,0:T(8,128)(2,1)S(1)} collective-permute-done((bf16[2,32,1536]{2,1,0:T(8,128)(2,1)S(1)}, bf16[2,32,1536]{2,1,0:T(8,128)(2,1)S(1)}, u32[]{:S(2)}, u32[]{:S(2)}) %collective-permute-start.7) | collective-permute-done | bytes 196640 | tf_op jit(solution)/shard_map/ppermute | solution.py:217
  38.2 6.4 %collective-permute-done.8.refs_3_ = bf16[2,32,1536]{2,1,0:T(8,128)(2,1)S(1)} collective-permute-done((bf16[2,32,1536]{2,1,0:T(8,128)(2,1)S(1)}, bf16[2,32,1536]{2,1,0:T(8,128)(2,1)S(1)}, u32[]{:S(2)}, u32[]{:S(2)}) %collective-permute-start.8) | collective-permute-done | bytes 196640 | tf_op jit(solution)/shard_map/ppermute | solution.py:217
  44.6 2.1 %middle.3 = (bf16[2,32,1536]{2,1,0:T(8,128)(2,1)S(1)}, bf16[2,32,1536]{2,1,0:T(8,128)(2,1)S(1)}, bf16[2,32,1536]{2,1,0:T(8,128)(2,1)S(1)}, bf16[2,32,1536]{2,1,0...) custom-call(bf16[2,256,256]{2,1,0:T(8,128)(2,1)S(1)} %copy-done.4, ...), custom_call_target="tpu_custom_call" | custom-call | flops 603979776 | bytes 2097152 | tf_op jit(solution)/shard_map/middle/pallas_call | solution.py:116
  46.7 0.1 collective-permute-start.12
  46.8 1.3 %collective-permute-start.13 = (bf16[2,32,1536]{2,1,0:T(8,128)(2,1)S(1)}, bf16[2,32,1536]{2,1,0:T(8,128)(2,1)S(1)}, u32[]{:S(2)}, u32[]{:S(2)}) collective-permute-start(bf16[2,32,1536]{2,1,0:T(8,128)(2,1)S(1)} %get-tuple-element.66), channel_id=1, source_target_pairs={{0,8},{4,12},{8,0},{12,4},{1,9},{5,13},{9,1},{13,5},{2,10},{6,14},... | collective-permute-start | bytes 589832 | tf_op jit(solution)/shard_map/ppermute | solution.py:217
  48.1 0.0 collective-permute-done.3.refs_1_
  48.1 1.3 %collective-permute-start.14 = (bf16[2,32,1536]{2,1,0:T(8,128)(2,1)S(1)}, bf16[2,32,1536]{2,1,0:T(8,128)(2,1)S(1)}, u32[]{:S(2)}, u32[]{:S(2)}) collective-permute-start(bf16[2,32,1536]{2,1,0:T(8,128)(2,1)S(1)} %get-tuple-element.67), channel_id=1, source_target_pairs={{0,12},{4,8},{8,4},{12,0},{1,13},{5,9},{9,5},{13,1},{2,14},{6,10},... | collective-permute-start | bytes 589832 | tf_op jit(solution)/shard_map/ppermute | solution.py:217
  49.4 0.4 collective-permute-done.4.refs_2_
  49.9 15.8 %collective-permute-done.5.refs_3_ = bf16[2,32,1536]{2,1,0:T(8,128)(2,1)S(1)} collective-permute-done((bf16[2,32,1536]{2,1,0:T(8,128)(2,1)S(1)}, bf16[2,32,1536]{2,1,0:T(8,128)(2,1)S(1)}, u32[]{:S(2)}, u32[]{:S(2)}) %collective-permute-start.5) | collective-permute-done | bytes 196640 | tf_op jit(solution)/shard_map/ppermute | solution.py:217
  65.7 0.0 copy-done.1
  65.7 0.4 left_terms.2
  66.1 3.3 %collective-permute-start.9 = (f32[3,64,256]{2,1,0:T(8,128)S(1)}, f32[3,64,256]{2,1,0:T(8,128)S(1)}, u32[]{:S(2)}, u32[]{:S(2)}) collective-permute-start(f32[3,64,256]{2,1,0:T(8,128)S(1)} %get-tuple-element.60), channel_id=1, source_target_pairs={{0,1},{1,0},{2,3},{3,2},{4,5},{5,4},{6,7},{7,6},{8,9},{9,8},{10,11... | collective-permute-start | bytes 589832 | tf_op jit(solution)/shard_map/ppermute | solution.py:217
  69.4 1.2 %collective-permute-start.10 = (f32[3,64,256]{2,1,0:T(8,128)S(1)}, f32[3,64,256]{2,1,0:T(8,128)S(1)}, u32[]{:S(2)}, u32[]{:S(2)}) collective-permute-start(f32[3,64,256]{2,1,0:T(8,128)S(1)} %get-tuple-element.61), channel_id=1, source_target_pairs={{0,2},{1,3},{2,0},{3,1},{4,6},{5,7},{6,4},{7,5},{8,10},{9,11},{10,... | collective-permute-start | bytes 589832 | tf_op jit(solution)/shard_map/ppermute | solution.py:217
  70.6 0.0 collective-permute-done.12.refs_1_
  70.6 0.5 collective-permute-start.11
  71.1 0.0 collective-permute-done.13.refs_2_
  71.1 3.0 %collective-permute-done.14.refs_3_ = bf16[2,32,1536]{2,1,0:T(8,128)(2,1)S(1)} collective-permute-done((bf16[2,32,1536]{2,1,0:T(8,128)(2,1)S(1)}, bf16[2,32,1536]{2,1,0:T(8,128)(2,1)S(1)}, u32[]{:S(2)}, u32[]{:S(2)}) %collective-permute-start.14) | collective-permute-done | bytes 196640 | tf_op jit(solution)/shard_map/ppermute | solution.py:217
  74.1 0.4 left_terms.3
  74.5 1.9 %collective-permute-start.15 = (f32[1,64,256]{2,1,0:T(8,128)S(1)}, f32[1,64,256]{2,1,0:T(8,128)S(1)}, u32[]{:S(2)}, u32[]{:S(2)}) collective-permute-start(f32[1,64,256]{2,1,0:T(8,128)S(1)} %get-tuple-element.69), channel_id=1, source_target_pairs={{0,1},{1,0},{2,3},{3,2},{4,5},{5,4},{6,7},{7,6},{8,9},{9,8},{10,11... | collective-permute-start | bytes 196616 | tf_op jit(solution)/shard_map/ppermute | solution.py:217
  76.4 1.2 %collective-permute-start.16 = (f32[1,64,256]{2,1,0:T(8,128)S(1)}, f32[1,64,256]{2,1,0:T(8,128)S(1)}, u32[]{:S(2)}, u32[]{:S(2)}) collective-permute-start(f32[1,64,256]{2,1,0:T(8,128)S(1)} %get-tuple-element.70), channel_id=1, source_target_pairs={{0,2},{1,3},{2,0},{3,1},{4,6},{5,7},{6,4},{7,5},{8,10},{9,11},{10,... | collective-permute-start | bytes 196616 | tf_op jit(solution)/shard_map/ppermute | solution.py:217
  77.6 0.0 collective-permute-done.15.refs_5_
  77.6 1.1 %collective-permute-start.17 = (f32[1,64,256]{2,1,0:T(8,128)S(1)}, f32[1,64,256]{2,1,0:T(8,128)S(1)}, u32[]{:S(2)}, u32[]{:S(2)}) collective-permute-start(f32[1,64,256]{2,1,0:T(8,128)S(1)} %get-tuple-element.71), channel_id=1, source_target_pairs={{0,3},{1,2},{2,1},{3,0},{4,7},{5,6},{6,5},{7,4},{8,11},{9,10},{10,... | collective-permute-start | bytes 196616 | tf_op jit(solution)/shard_map/ppermute | solution.py:217
  78.7 2.7 %collective-permute-done.16.refs_6_ = f32[1,64,256]{2,1,0:T(8,128)S(1)} collective-permute-done((f32[1,64,256]{2,1,0:T(8,128)S(1)}, f32[1,64,256]{2,1,0:T(8,128)S(1)}, u32[]{:S(2)}, u32[]{:S(2)}) %collective-permute-start.16) | collective-permute-done | bytes 65568 | tf_op jit(solution)/shard_map/ppermute | solution.py:217
  81.5 1.6 %collective-permute-done.17.refs_7_ = f32[1,64,256]{2,1,0:T(8,128)S(1)} collective-permute-done((f32[1,64,256]{2,1,0:T(8,128)S(1)}, f32[1,64,256]{2,1,0:T(8,128)S(1)}, u32[]{:S(2)}, u32[]{:S(2)}) %collective-permute-start.17) | collective-permute-done | bytes 65568 | tf_op jit(solution)/shard_map/ppermute | solution.py:217
  83.0 0.0 collective-permute-done.9.refs_1_
  83.0 0.0 collective-permute-done.10.refs_2_
  83.1 0.0 collective-permute-done.11.refs_3_
  83.1 0.7 finish.1
Async XLA Ops:
  0.6 1.4 %copy-start = (bf16[1536,512]{1,0:T(8,128)(2,1)S(1)}, bf16[1536,512]{1,0:T(8,128)(2,1)}, u32[]{:S(2)}) copy-start(bf16[1536,512]{1,0:T(8,128)(2,1)} %x_ref.6) | copy-start | bytes 4718596
  2.0 0.9 %copy-start.3 = (bf16[2,256,256]{2,1,0:T(8,128)(2,1)S(1)}, bf16[2,256,256]{2,1,0:T(8,128)(2,1)}, u32[]{:S(2)}) copy-start(bf16[2,256,256]{2,1,0:T(8,128)(2,1)} %left_ref.2) | copy-start | bytes 786436
  3.0 21.6 %copy-start.2 = (bf16[1536,512]{1,0:T(8,128)(2,1)S(1)}, bf16[1536,512]{1,0:T(8,128)(2,1)}, u32[]{:S(2)}) copy-start(bf16[1536,512]{1,0:T(8,128)(2,1)} %targets_ref.3) | copy-start | bytes 4718596
  3.0 21.6 %copy-start.4 = (bf16[2,256,256]{2,1,0:T(8,128)(2,1)S(1)}, bf16[2,256,256]{2,1,0:T(8,128)(2,1)}, u32[]{:S(2)}) copy-start(bf16[2,256,256]{2,1,0:T(8,128)(2,1)} %right_ref.2) | copy-start | bytes 786436
  4.0 7.7 %collective-permute-start = (bf16[2,32,1536]{2,1,0:T(8,128)(2,1)S(1)}, bf16[2,32,1536]{2,1,0:T(8,128)(2,1)S(1)}, u32[]{:S(2)}, u32[]{:S(2)}) collective-permute-start(bf16[2,32,1536]{2,1,0:T(8,128)(2,1)S(1)} %get-tuple-element.38), channel_id=1, source_target_pairs={{0,4},{4,0},{8,12},{12,8},{1,5},{5,1},{9,13},{13,9},{2,6},{6,2},{1... | collective-permute-start | bytes 589832 | tf_op jit(solution)/shard_map/ppermute | solution.py:217
  5.4 8.6 %collective-permute-start.1 = (bf16[2,32,1536]{2,1,0:T(8,128)(2,1)S(1)}, bf16[2,32,1536]{2,1,0:T(8,128)(2,1)S(1)}, u32[]{:S(2)}, u32[]{:S(2)}) collective-permute-start(bf16[2,32,1536]{2,1,0:T(8,128)(2,1)S(1)} %get-tuple-element.39), channel_id=1, source_target_pairs={{0,8},{4,12},{8,0},{12,4},{1,9},{5,13},{9,1},{13,5},{2,10},{6,14},... | collective-permute-start | bytes 589832 | tf_op jit(solution)/shard_map/ppermute | solution.py:217
  5.4 19.1 %collective-permute-start.2 = (bf16[2,32,1536]{2,1,0:T(8,128)(2,1)S(1)}, bf16[2,32,1536]{2,1,0:T(8,128)(2,1)S(1)}, u32[]{:S(2)}, u32[]{:S(2)}) collective-permute-start(bf16[2,32,1536]{2,1,0:T(8,128)(2,1)S(1)} %get-tuple-element.40), channel_id=1, source_target_pairs={{0,12},{4,8},{8,4},{12,0},{1,13},{5,9},{9,5},{13,1},{2,14},{6,10},... | collective-permute-start | bytes 589832 | tf_op jit(solution)/shard_map/ppermute | solution.py:217
  7.8 19.3 %collective-permute-start.6 = (bf16[2,32,1536]{2,1,0:T(8,128)(2,1)S(1)}, bf16[2,32,1536]{2,1,0:T(8,128)(2,1)S(1)}, u32[]{:S(2)}, u32[]{:S(2)}) collective-permute-start(bf16[2,32,1536]{2,1,0:T(8,128)(2,1)S(1)} %get-tuple-element.52), channel_id=1, source_target_pairs={{0,4},{4,0},{8,12},{12,8},{1,5},{5,1},{9,13},{13,9},{2,6},{6,2},{1... | collective-permute-start | bytes 589832 | tf_op jit(solution)/shard_map/ppermute | solution.py:217
  10.0 28.2 %collective-permute-start.7 = (bf16[2,32,1536]{2,1,0:T(8,128)(2,1)S(1)}, bf16[2,32,1536]{2,1,0:T(8,128)(2,1)S(1)}, u32[]{:S(2)}, u32[]{:S(2)}) collective-permute-start(bf16[2,32,1536]{2,1,0:T(8,128)(2,1)S(1)} %get-tuple-element.53), channel_id=1, source_target_pairs={{0,8},{4,12},{8,0},{12,4},{1,9},{5,13},{9,1},{13,5},{2,10},{6,14},... | collective-permute-start | bytes 589832 | tf_op jit(solution)/shard_map/ppermute | solution.py:217
  11.7 32.9 %collective-permute-start.8 = (bf16[2,32,1536]{2,1,0:T(8,128)(2,1)S(1)}, bf16[2,32,1536]{2,1,0:T(8,128)(2,1)S(1)}, u32[]{:S(2)}, u32[]{:S(2)}) collective-permute-start(bf16[2,32,1536]{2,1,0:T(8,128)(2,1)S(1)} %get-tuple-element.54), channel_id=1, source_target_pairs={{0,12},{4,8},{8,4},{12,0},{1,13},{5,9},{9,5},{13,1},{2,14},{6,10},... | collective-permute-start | bytes 589832 | tf_op jit(solution)/shard_map/ppermute | solution.py:217
  26.7 39.0 %copy-start.1 = (bf16[1536,512]{1,0:T(8,128)(2,1)S(1)}, bf16[1536,512]{1,0:T(8,128)(2,1)}, u32[]{:S(2)}) copy-start(bf16[1536,512]{1,0:T(8,128)(2,1)} %x_ref.6) | copy-start | bytes 4718596
  26.7 21.5 %collective-permute-start.3 = (bf16[2,32,1536]{2,1,0:T(8,128)(2,1)S(1)}, bf16[2,32,1536]{2,1,0:T(8,128)(2,1)S(1)}, u32[]{:S(2)}, u32[]{:S(2)}) collective-permute-start(bf16[2,32,1536]{2,1,0:T(8,128)(2,1)S(1)} %get-tuple-element.42), channel_id=1, source_target_pairs={{0,4},{4,0},{8,12},{12,8},{1,5},{5,1},{9,13},{13,9},{2,6},{6,2},{1... | collective-permute-start | bytes 589832 | tf_op jit(solution)/shard_map/ppermute | solution.py:217
  26.7 23.1 %collective-permute-start.4 = (bf16[2,32,1536]{2,1,0:T(8,128)(2,1)S(1)}, bf16[2,32,1536]{2,1,0:T(8,128)(2,1)S(1)}, u32[]{:S(2)}, u32[]{:S(2)}) collective-permute-start(bf16[2,32,1536]{2,1,0:T(8,128)(2,1)S(1)} %get-tuple-element.43), channel_id=1, source_target_pairs={{0,8},{4,12},{8,0},{12,4},{1,9},{5,13},{9,1},{13,5},{2,10},{6,14},... | collective-permute-start | bytes 589832 | tf_op jit(solution)/shard_map/ppermute | solution.py:217
  27.0 38.6 %collective-permute-start.5 = (bf16[2,32,1536]{2,1,0:T(8,128)(2,1)S(1)}, bf16[2,32,1536]{2,1,0:T(8,128)(2,1)S(1)}, u32[]{:S(2)}, u32[]{:S(2)}) collective-permute-start(bf16[2,32,1536]{2,1,0:T(8,128)(2,1)S(1)} %get-tuple-element.44), channel_id=1, source_target_pairs={{0,12},{4,8},{8,4},{12,0},{1,13},{5,9},{9,5},{13,1},{2,14},{6,10},... | collective-permute-start | bytes 589832 | tf_op jit(solution)/shard_map/ppermute | solution.py:217
  46.7 23.9 %collective-permute-start.12 = (bf16[2,32,1536]{2,1,0:T(8,128)(2,1)S(1)}, bf16[2,32,1536]{2,1,0:T(8,128)(2,1)S(1)}, u32[]{:S(2)}, u32[]{:S(2)}) collective-permute-start(bf16[2,32,1536]{2,1,0:T(8,128)(2,1)S(1)} %get-tuple-element.65), channel_id=1, source_target_pairs={{0,4},{4,0},{8,12},{12,8},{1,5},{5,1},{9,13},{13,9},{2,6},{6,2},{1... | collective-permute-start | bytes 589832 | tf_op jit(solution)/shard_map/ppermute | solution.py:217
  46.8 24.3 %collective-permute-start.13 = (bf16[2,32,1536]{2,1,0:T(8,128)(2,1)S(1)}, bf16[2,32,1536]{2,1,0:T(8,128)(2,1)S(1)}, u32[]{:S(2)}, u32[]{:S(2)}) collective-permute-start(bf16[2,32,1536]{2,1,0:T(8,128)(2,1)S(1)} %get-tuple-element.66), channel_id=1, source_target_pairs={{0,8},{4,12},{8,0},{12,4},{1,9},{5,13},{9,1},{13,5},{2,10},{6,14},... | collective-permute-start | bytes 589832 | tf_op jit(solution)/shard_map/ppermute | solution.py:217
  48.1 26.0 %collective-permute-start.14 = (bf16[2,32,1536]{2,1,0:T(8,128)(2,1)S(1)}, bf16[2,32,1536]{2,1,0:T(8,128)(2,1)S(1)}, u32[]{:S(2)}, u32[]{:S(2)}) collective-permute-start(bf16[2,32,1536]{2,1,0:T(8,128)(2,1)S(1)} %get-tuple-element.67), channel_id=1, source_target_pairs={{0,12},{4,8},{8,4},{12,0},{1,13},{5,9},{9,5},{13,1},{2,14},{6,10},... | collective-permute-start | bytes 589832 | tf_op jit(solution)/shard_map/ppermute | solution.py:217
  66.1 17.0 %collective-permute-start.9 = (f32[3,64,256]{2,1,0:T(8,128)S(1)}, f32[3,64,256]{2,1,0:T(8,128)S(1)}, u32[]{:S(2)}, u32[]{:S(2)}) collective-permute-start(f32[3,64,256]{2,1,0:T(8,128)S(1)} %get-tuple-element.60), channel_id=1, source_target_pairs={{0,1},{1,0},{2,3},{3,2},{4,5},{5,4},{6,7},{7,6},{8,9},{9,8},{10,11... | collective-permute-start | bytes 589832 | tf_op jit(solution)/shard_map/ppermute | solution.py:217
  69.4 13.7 %collective-permute-start.10 = (f32[3,64,256]{2,1,0:T(8,128)S(1)}, f32[3,64,256]{2,1,0:T(8,128)S(1)}, u32[]{:S(2)}, u32[]{:S(2)}) collective-permute-start(f32[3,64,256]{2,1,0:T(8,128)S(1)} %get-tuple-element.61), channel_id=1, source_target_pairs={{0,2},{1,3},{2,0},{3,1},{4,6},{5,7},{6,4},{7,5},{8,10},{9,11},{10,... | collective-permute-start | bytes 589832 | tf_op jit(solution)/shard_map/ppermute | solution.py:217
  70.6 12.4 %collective-permute-start.11 = (f32[3,64,256]{2,1,0:T(8,128)S(1)}, f32[3,64,256]{2,1,0:T(8,128)S(1)}, u32[]{:S(2)}, u32[]{:S(2)}) collective-permute-start(f32[3,64,256]{2,1,0:T(8,128)S(1)} %get-tuple-element.62), channel_id=1, source_target_pairs={{0,3},{1,2},{2,1},{3,0},{4,7},{5,6},{6,5},{7,4},{8,11},{9,10},{10,... | collective-permute-start | bytes 589832 | tf_op jit(solution)/shard_map/ppermute | solution.py:217
  74.5 3.1 %collective-permute-start.15 = (f32[1,64,256]{2,1,0:T(8,128)S(1)}, f32[1,64,256]{2,1,0:T(8,128)S(1)}, u32[]{:S(2)}, u32[]{:S(2)}) collective-permute-start(f32[1,64,256]{2,1,0:T(8,128)S(1)} %get-tuple-element.69), channel_id=1, source_target_pairs={{0,1},{1,0},{2,3},{3,2},{4,5},{5,4},{6,7},{7,6},{8,9},{9,8},{10,11... | collective-permute-start | bytes 196616 | tf_op jit(solution)/shard_map/ppermute | solution.py:217
  76.4 5.1 %collective-permute-start.16 = (f32[1,64,256]{2,1,0:T(8,128)S(1)}, f32[1,64,256]{2,1,0:T(8,128)S(1)}, u32[]{:S(2)}, u32[]{:S(2)}) collective-permute-start(f32[1,64,256]{2,1,0:T(8,128)S(1)} %get-tuple-element.70), channel_id=1, source_target_pairs={{0,2},{1,3},{2,0},{3,1},{4,6},{5,7},{6,4},{7,5},{8,10},{9,11},{10,... | collective-permute-start | bytes 196616 | tf_op jit(solution)/shard_map/ppermute | solution.py:217
  77.6 5.4 %collective-permute-start.17 = (f32[1,64,256]{2,1,0:T(8,128)S(1)}, f32[1,64,256]{2,1,0:T(8,128)S(1)}, u32[]{:S(2)}, u32[]{:S(2)}) collective-permute-start(f32[1,64,256]{2,1,0:T(8,128)S(1)} %get-tuple-element.71), channel_id=1, source_target_pairs={{0,3},{1,2},{2,1},{3,0},{4,7},{5,6},{6,5},{7,4},{8,11},{9,10},{10,... | collective-permute-start | bytes 196616 | tf_op jit(solution)/shard_map/ppermute | solution.py:217

commit v3 on v2

--- a/solution.py
+++ b/solution.py
@@ -8,6 +8,7 @@
 from jax.sharding import PartitionSpec as P
 
 F32, BF16 = jnp.float32, jnp.bfloat16
+ORDERS = ((2, 3, 1), (1, 2, 3)), ((2, 3, 1), (1, 2, 3))
 NT = (((1,), (1,)), ((), ()))
 NN = (((1,), (0,)), ((), ()))
 TN = (((0,), (0,)), ((), ()))
@@ -19,6 +20,11 @@
 
 def after(value, *others):
     return lax.optimization_barrier((value, others))[0]
+
+
+def listed(kind, peers, g):
+    first = [d for d in ORDERS[kind][g % 2] if d < peers]
+    return first + [d for d in range(peers) if d not in first]
 
 
 def call(kernel, name, flops, **kwargs):
@@ -34,48 +40,67 @@
     )
 
 
+def in_hbm(value):
+    return pltpu.with_memory_space_constraint(value, pltpu.HBM)
+
+
 def whole(shape):
     return pl.BlockSpec(shape, lambda i: (0,) * len(shape))
 
 
-def forward_kernel(peers, g, left_ref, x_ref, *refs):
-    outs, held = refs[:peers], refs[peers]
+def forward_kernel(peers, g, tiles, left_ref, x_ref, *refs):
+    outs, (held, whole_left, rows_in, left_sem, row_sems) = refs[:peers], refs[peers:]
     blocks, width = left_ref.shape[0], left_ref.shape[1]
     rows = width // peers
     step = rows // blocks
+    tile = x_ref.shape[0] // tiles
     me = lax.axis_index("blk")
-
-    @pl.when(pl.program_id(0) == 0)
-    def _():
-        for d in range(peers):
-            at = pl.multiple_of((me ^ d) * rows + g * step, step)
-            for k in range(blocks):
-                held[k, d * step : (d + 1) * step, :] = left_ref[k, pl.ds(at, step), :]
-
-    for k in range(blocks):
-        first = dot(held[k], x_ref[:, k * width : (k + 1) * width], NT).astype(BF16)
-        for d in range(peers):
-            outs[d][k] = first[d * step : (d + 1) * step]
-
-
-def forward(left, x, peers, g, tile):
+    fetch = pltpu.make_async_copy(left_ref, whole_left, left_sem)
+    fetch.start()
+    loads = []
+    for n in range(tiles):
+        at = pl.ds(n * tile, tile)
+        loads.append(pltpu.make_async_copy(x_ref.at[at], rows_in.at[at], row_sems.at[n]))
+        loads[-1].start()
+    fetch.wait()
+    for d in range(peers):
+        at = pl.multiple_of((me ^ d) * rows + g * step, step)
+        for k in range(blocks):
+            held[k, d * step : (d + 1) * step, :] = whole_left[k, pl.ds(at, step), :]
+    for n in range(tiles):
+        loads[n].wait()
+        low = n * tile
+        for k in range(blocks):
+            part = rows_in[low : low + tile, k * width : (k + 1) * width]
+            first = dot(held[k], part, NT).astype(BF16)
+            for d in range(peers):
+                outs[d][k, :, low : low + tile] = first[d * step : (d + 1) * step]
+
+
+def forward(left, x, peers, g, tiles):
     blocks, width, _ = left.shape
     step = width // peers // blocks
     tokens = x.shape[0]
     return call(
-        functools.partial(forward_kernel, peers, g),
+        functools.partial(forward_kernel, peers, g, tiles),
         "forward",
         2 * tokens * width * width,
-        grid=(tokens // tile,),
-        in_specs=[whole(left.shape), pl.BlockSpec((tile, x.shape[1]), lambda i: (i, 0))],
-        out_specs=[pl.BlockSpec((blocks, step, tile), lambda i: (0, 0, i))] * peers,
+        in_specs=[pl.BlockSpec(memory_space=pltpu.HBM)] * 2,
+        out_specs=[pl.BlockSpec(memory_space=pltpu.VMEM)] * peers,
         out_shape=[jax.ShapeDtypeStruct((blocks, step, tokens), BF16)] * peers,
-        scratch_shapes=[pltpu.VMEM((blocks, peers * step, width), BF16)],
-    )(left, x)
-
-
-def middle_kernel(peers, toks, g, right_ref, targets_ref, *refs):
+        scratch_shapes=[
+            pltpu.VMEM((blocks, peers * step, width), BF16),
+            pltpu.VMEM(left.shape, BF16),
+            pltpu.VMEM(x.shape, BF16),
+            pltpu.SemaphoreType.DMA,
+            pltpu.SemaphoreType.DMA((tiles,)),
+        ],
+    )(in_hbm(left), in_hbm(x))
+
+
+def middle_kernel(peers, toks, g, order, right_ref, targets_ref, *refs):
     pieces, backs, terms = refs[:peers], refs[peers : 2 * peers], refs[2 * peers : 2 * peers + toks]
+    pieces = [pieces[order.index(d)] for d in range(peers)]
     mixed, back, total = refs[2 * peers + toks :]
     blocks, step, _ = pieces[0].shape
     width = right_ref.shape[1]
@@ -109,12 +134,13 @@
 
 def middle(right, targets, pieces, toks, g, tile):
     peers = len(pieces)
+    order = listed(0, peers, g)
     blocks, step, tokens = pieces[0].shape
     width = right.shape[1]
     piece = pl.BlockSpec((blocks, step, tile), lambda i: (0, 0, i))
     term = (width // toks, width)
     return call(
-        functools.partial(middle_kernel, peers, toks, g),
+        functools.partial(middle_kernel, peers, toks, g, order),
         "middle",
         6 * tokens * width * width,
         grid=(tokens // tile,),
@@ -128,14 +154,15 @@
             pltpu.VMEM((width, tile), BF16),
             pltpu.VMEM((width, width), F32),
         ],
-    )(right, targets, *pieces)
-
-
-def left_kernel(peers, toks, carried, x_ref, *refs):
-    pieces, refs = refs[:peers], refs[peers:]
+    )(right, in_hbm(targets), *[pieces[d] for d in order])
+
+
+def left_kernel(peers, toks, carried, order, x_ref, *refs):
+    pieces, refs = [refs[order.index(d)] for d in range(peers)], refs[peers:]
     extras, outs, (joined, partial) = refs[: carried * toks], refs[carried * toks : -2], refs[-2:]
     blocks, step, _ = pieces[0].shape
     width = x_ref.shape[1] // blocks
+    parts = len(outs)
     mine = lax.axis_index("blk") ^ lax.axis_index("tok")
     for k in range(blocks):
         for d in range(peers):
@@ -144,60 +171,75 @@
     for s in range(toks):
         at = pl.multiple_of((mine ^ s) * step, step)
         for k in range(blocks):
-            outs[s][carried, k * step : (k + 1) * step, :] = partial[k, pl.ds(at, step), :]
+            outs[s % parts][s // parts, carried, k * step : (k + 1) * step, :] = partial[k, pl.ds(at, step), :]
         for n in range(carried):
-            outs[s][n] = extras[n * toks + s][...]
-
-
-def left_terms(x, pieces, extras, toks):
+            outs[s % parts][s // parts, n] = extras[n * toks + s][...]
+
+
+def left_terms(x, pieces, extras, toks, parts, g):
     peers = len(pieces)
+    order = listed(1, peers, g)
     blocks, step, tokens = pieces[0].shape
     width = x.shape[1] // blocks
     carried = len(extras)
     flat = [e[s] for e in extras for s in range(toks)]
     return call(
-        functools.partial(left_kernel, peers, toks, carried),
+        functools.partial(left_kernel, peers, toks, carried, order),
         "left_terms",
         2 * tokens * width * width,
         in_specs=[pl.BlockSpec(memory_space=pltpu.VMEM)] * (1 + peers + len(flat)),
-        out_specs=[pl.BlockSpec(memory_space=pltpu.VMEM)] * toks,
-        out_shape=[jax.ShapeDtypeStruct((carried + 1, blocks * step, width), F32)] * toks,
+        out_specs=[pl.BlockSpec(memory_space=pltpu.VMEM)] * parts,
+        out_shape=[jax.ShapeDtypeStruct((toks // parts, carried + 1, blocks * step, width), F32)]
+        * parts,
         scratch_shapes=[
             pltpu.VMEM((peers * step, tokens), BF16),
             pltpu.VMEM((blocks, peers * step, width), F32),
         ],
-    )(x, *pieces, *flat)
-
-
-def finish_kernel(toks, groups, scale, *refs):
-    sums = refs[: toks * groups]
-    left_out, right_out = refs[toks * groups :]
+    )(x, *[pieces[d] for d in order], *flat)
+
+
+def fold_kernel(keep_ref, got_ref, keep_out, send_out):
+    for n in range(keep_ref.shape[0]):
+        (send_out if n % 2 else keep_out)[n // 2] = keep_ref[n] + got_ref[n]
+
+
+def fold(keep, got):
+    half = jax.ShapeDtypeStruct((keep.shape[0] // 2,) + keep.shape[1:], F32)
+    return call(
+        fold_kernel,
+        "fold",
+        1,
+        in_specs=[pl.BlockSpec(memory_space=pltpu.VMEM)] * 2,
+        out_specs=[pl.BlockSpec(memory_space=pltpu.VMEM)] * 2,
+        out_shape=[half] * 2,
+    )(keep, got)
+
+
+def finish_kernel(counts, scale, *refs):
+    left_out, right_out = refs[sum(counts) :]
     blocks, rows, _ = left_out.shape
-    step = rows // groups
-    for g in range(groups):
-        parts = sums[g * toks : (g + 1) * toks]
-        last = parts[0].shape[0] - 1
-        total = parts[0][last]
-        for p in parts[1:]:
-            total = total + p[last]
-        total = total * scale
-        for k in range(blocks):
-            left_out[k, g * step : (g + 1) * step, :] = total[k * step : (k + 1) * step]
-        if last:
-            for n in range(last):
-                total = parts[0][n]
-                for p in parts[1:]:
-                    total = total + p[n]
-                right_out[n] = total * scale
+    step = rows // len(counts)
+    for g, count in enumerate(counts):
+        parts, refs = refs[:count], refs[count:]
+        last = parts[0].shape[1] - 1
+        for n in range(last + 1):
+            total = parts[0][0, n]
+            for p in parts[1:]:
+                total = total + p[0, n]
+            total = total * scale
+            if n < last:
+                right_out[n] = total
+            else:
+                for k in range(blocks):
+                    left_out[k, g * step : (g + 1) * step, :] = total[k * step : (k + 1) * step]
 
 
 def finish(groups, blocks, scale):
-    toks = len(groups[0])
-    _, rows, width = groups[0][0].shape
+    _, _, rows, width = groups[0][0].shape
     flat = [a for group in groups for a in group]
     shape = jax.ShapeDtypeStruct((blocks, rows, width), F32)
     return call(
-        functools.partial(finish_kernel, toks, len(groups), scale),
+        functools.partial(finish_kernel, [len(group) for group in groups], scale),
         "finish",
         1,
         in_specs=[pl.BlockSpec(memory_space=pltpu.VMEM)] * len(flat),
@@ -223,7 +265,7 @@
 
     left, arrived = left_factor, []
     for g in range(blocks):
-        sent = forward(left, inputs, peers, g, tile)
+        sent = forward(left, inputs, peers, g, 2)
         left = after(left_factor, *sent)
         arrived.append(exchange("blk", sent))
 
@@ -234,12 +276,23 @@
         returned.append(exchange("blk", res[:peers]))
         terms.append(res[peers:])
 
-    rows, sums = inputs, []
+    rows, groups = inputs, []
     for g in range(blocks):
-        out = left_terms(rows, returned[g], terms if g == 0 else [], toks)
+        last = g == blocks - 1
+        extras = terms if g == 0 else []
+        out = left_terms(rows, returned[g], extras, toks, 2 if last else toks, g)
         rows = after(inputs, *out)
-        sums.append(exchange("tok", out))
-    return tuple(finish(sums, blocks, 1.0 / tokens))
+        if last:
+            keep, send = out
+            got, hop = swap("tok", toks, 1, send), 2
+            got = after(got, *groups[0]) if toks > 2 else got
+            while hop < toks:
+                keep, send = fold(keep, got)
+                got, hop = swap("tok", toks, hop, send), 2 * hop
+            groups.append([keep, got])
+        else:
+            groups.append(exchange("tok", out))
+    return tuple(finish(groups, blocks, 1.0 / tokens))
 
 
 def solution(mesh):

time: 84.1 us -> 80.8 us (0.961)
  waiting for transfers between devices: 53.3 us -> 47.9 us
  Pallas kernels: 7.77 us -> 12 us
  local copies, waits for them, and re-layouts: 2.37 us -> 0.01 us
    ppermute x18 -> x17, waiting for transfers between devices: 53.3 us -> 47.9 us  [swap(): return lax.ppermute(value, axis, [(j, j ^ d) for j in range(size)])]
    pallas_call x7 -> x8, Pallas kernels: 7.77 us -> 12 us  [the longest x2 6.34 us: middle(): call(functools.partial(middle_kernel, peers, toks, g, order), 'middle', 6...]
    unnamed x10 -> x4, local copies, waits for them, and re-layouts: 2.37 us -> 0.01 us
    ppermute x18 -> x17, starting transfers between devices: 19.6 us -> 19.1 us  [swap(): return lax.ppermute(value, axis, [(j, j ^ d) for j in range(size)])]
  transfers between devices with their start and end apart: 18 -> 17, of which waited for: 10 -> 8; matrix products, arithmetic and copies ran while one was open for 0% -> 0% of each run, Pallas kernels for 7% -> 11%
where the time goes in v3:
time: 80.8 us; the launch traced here: 79.7 us
  waiting for transfers between devices  47.9 us (59%)
  starting transfers between devices  19.1 us (24%)
  Pallas kernels  12 us (15%)
    ppermute x17, waiting for transfers between devices, swap(): return lax.ppermute(value, axis, [(j, j ^ d) for j in range(size)])  47.9 us
    ppermute x17, starting transfers between devices, swap(): return lax.ppermute(value, axis, [(j, j ^ d) for j in range(size)])  19.1 us
    pallas_call x2, Pallas kernels, middle(): call(functools.partial(middle_kernel, peers, toks, g, order), 'middle', 6...  6.34 us
    pallas_call x2, Pallas kernels, forward(): call(functools.partial(forward_kernel, peers, g, tiles), 'forward', 2 * t...  4.06 us
  transfers between devices with their start and end apart: 17, of which 8 were waited for; matrix products, arithmetic and copies ran while one was open for 0% of the time, Pallas kernels for 11%

profile of v3, /device:TPU:21, one launch (start us, length us, event | category | flops | bytes accessed | tf_op | source)
XLA Modules:
  0.0 79.7 jit_solution(17838988482557036861)
XLA Ops:
  0.6 0.0 copy-start.1
  0.6 2.1 %forward.2 = (bf16[2,32,1536]{2,1,0:T(8,128)(2,1)S(1)}, bf16[2,32,1536]{2,1,0:T(8,128)(2,1)S(1)}, bf16[2,32,1536]{2,1,0:T(8,128)(2,1)S(1)}, bf16[2,32,1536]{2,1,0:T(8,128)(2,1)S(1)}) custom-call(bf16[2,256,256]{2,1,0:T(8,128)(2,1)} %left_ref.2, bf16[1536,512]{1,0:T(8,128)(2,1)} %x_ref.6), custom_call_target="tpu_custom_call" | custom-call | flops 201326592 | bytes 1572864 | tf_op jit(solution)/shard_map/forward/pallas_call | solution.py:84
  2.7 0.1 collective-permute-start
  2.8 2.4 %collective-permute-start.1 = (bf16[2,32,1536]{2,1,0:T(8,128)(2,1)S(1)}, bf16[2,32,1536]{2,1,0:T(8,128)(2,1)S(1)}, u32[]{:S(2)}, u32[]{:S(2)}) collective-permute-start(bf16[2,32,1536]{2,1,0:T(8,128)(2,1)S(1)} %get-tuple-element.39), channel_id=1, source_target_pairs={{0,12},{4,8},{8,4},{12,0},{1,13},{5,9},{9,5},{13,1},{2,14},{6,10},... | collective-permute-start | bytes 589832 | tf_op jit(solution)/shard_map/ppermute | solution.py:259
  5.2 1.1 %collective-permute-start.2 = (bf16[2,32,1536]{2,1,0:T(8,128)(2,1)S(1)}, bf16[2,32,1536]{2,1,0:T(8,128)(2,1)S(1)}, u32[]{:S(2)}, u32[]{:S(2)}) collective-permute-start(bf16[2,32,1536]{2,1,0:T(8,128)(2,1)S(1)} %get-tuple-element.40), channel_id=1, source_target_pairs={{0,4},{4,0},{8,12},{12,8},{1,5},{5,1},{9,13},{13,9},{2,6},{6,2},{1... | collective-permute-start | bytes 589832 | tf_op jit(solution)/shard_map/ppermute | solution.py:259
  6.3 2.0 %forward.3 = (bf16[2,32,1536]{2,1,0:T(8,128)(2,1)S(1)}, bf16[2,32,1536]{2,1,0:T(8,128)(2,1)S(1)}, bf16[2,32,1536]{2,1,0:T(8,128)(2,1)S(1)}, bf16[2,32,1536]{2,1,0:T(8,128)(2,1)S(1)}) custom-call(bf16[2,256,256]{2,1,0:T(8,128)(2,1)} %left_ref.2, bf16[1536,512]{1,0:T(8,128)(2,1)} %x_ref.6), custom_call_target="tpu_custom_call" | custom-call | flops 201326592 | bytes 1572864 | tf_op jit(solution)/shard_map/forward/pallas_call | solution.py:84
  8.3 0.5 collective-permute-start.6
  8.8 1.0 %collective-permute-start.7 = (bf16[2,32,1536]{2,1,0:T(8,128)(2,1)S(1)}, bf16[2,32,1536]{2,1,0:T(8,128)(2,1)S(1)}, u32[]{:S(2)}, u32[]{:S(2)}) collective-permute-start(bf16[2,32,1536]{2,1,0:T(8,128)(2,1)S(1)} %get-tuple-element.53), channel_id=1, source_target_pairs={{0,8},{4,12},{8,0},{12,4},{1,9},{5,13},{9,1},{13,5},{2,10},{6,14},... | collective-permute-start | bytes 589832 | tf_op jit(solution)/shard_map/ppermute | solution.py:259
  9.8 5.1 %collective-permute-done.refs_0_ = bf16[2,32,1536]{2,1,0:T(8,128)(2,1)S(1)} collective-permute-done((bf16[2,32,1536]{2,1,0:T(8,128)(2,1)S(1)}, bf16[2,32,1536]{2,1,0:T(8,128)(2,1)S(1)}, u32[]{:S(2)}, u32[]{:S(2)}) %collective-permute-start) | collective-permute-done | bytes 196640 | tf_op jit(solution)/shard_map/ppermute | solution.py:259
  14.9 3.3 %collective-permute-start.8 = (bf16[2,32,1536]{2,1,0:T(8,128)(2,1)S(1)}, bf16[2,32,1536]{2,1,0:T(8,128)(2,1)S(1)}, u32[]{:S(2)}, u32[]{:S(2)}) collective-permute-start(bf16[2,32,1536]{2,1,0:T(8,128)(2,1)S(1)} %get-tuple-element.54), channel_id=1, source_target_pairs={{0,12},{4,8},{8,4},{12,0},{1,13},{5,9},{9,5},{13,1},{2,14},{6,10},... | collective-permute-start | bytes 589832 | tf_op jit(solution)/shard_map/ppermute | solution.py:259
  18.2 6.0 %collective-permute-done.1.refs_1_ = bf16[2,32,1536]{2,1,0:T(8,128)(2,1)S(1)} collective-permute-done((bf16[2,32,1536]{2,1,0:T(8,128)(2,1)S(1)}, bf16[2,32,1536]{2,1,0:T(8,128)(2,1)S(1)}, u32[]{:S(2)}, u32[]{:S(2)}) %collective-permute-start.1) | collective-permute-done | bytes 196640 | tf_op jit(solution)/shard_map/ppermute | solution.py:259
  24.2 0.0 collective-permute-done.2.refs_2_
  24.2 0.0 copy-done.1
  24.2 3.2 %middle.2 = (bf16[2,32,1536]{2,1,0:T(8,128)(2,1)S(1)}, bf16[2,32,1536]{2,1,0:T(8,128)(2,1)S(1)}, bf16[2,32,1536]{2,1,0:T(8,128)(2,1)S(1)}, bf16[2,32,1536]{2,1,0...) custom-call(bf16[2,256,256]{2,1,0:T(8,128)(2,1)S(1)} %copy-done.1, ...), custom_call_target="tpu_custom_call" | custom-call | flops 603979776 | bytes 2097152 | tf_op jit(solution)/shard_map/middle/pallas_call | solution.py:142
  27.4 0.0 copy-start
  27.4 0.1 collective-permute-start.3
  27.5 0.1 collective-permute-start.4
  27.5 0.0 collective-permute-done.6.refs_0_
  27.5 3.4 %collective-permute-start.5 = (bf16[2,32,1536]{2,1,0:T(8,128)(2,1)S(1)}, bf16[2,32,1536]{2,1,0:T(8,128)(2,1)S(1)}, u32[]{:S(2)}, u32[]{:S(2)}) collective-permute-start(bf16[2,32,1536]{2,1,0:T(8,128)(2,1)S(1)} %get-tuple-element.44), channel_id=1, source_target_pairs={{0,4},{4,0},{8,12},{12,8},{1,5},{5,1},{9,13},{13,9},{2,6},{6,2},{1... | collective-permute-start | bytes 589832 | tf_op jit(solution)/shard_map/ppermute | solution.py:259
  31.0 9.2 %collective-permute-done.7.refs_1_ = bf16[2,32,1536]{2,1,0:T(8,128)(2,1)S(1)} collective-permute-done((bf16[2,32,1536]{2,1,0:T(8,128)(2,1)S(1)}, bf16[2,32,1536]{2,1,0:T(8,128)(2,1)S(1)}, u32[]{:S(2)}, u32[]{:S(2)}) %collective-permute-start.7) | collective-permute-done | bytes 196640 | tf_op jit(solution)/shard_map/ppermute | solution.py:259
  40.2 8.3 %collective-permute-done.8.refs_2_ = bf16[2,32,1536]{2,1,0:T(8,128)(2,1)S(1)} collective-permute-done((bf16[2,32,1536]{2,1,0:T(8,128)(2,1)S(1)}, bf16[2,32,1536]{2,1,0:T(8,128)(2,1)S(1)}, u32[]{:S(2)}, u32[]{:S(2)}) %collective-permute-start.8) | collective-permute-done | bytes 196640 | tf_op jit(solution)/shard_map/ppermute | solution.py:259
  48.5 3.2 %middle.3 = (bf16[2,32,1536]{2,1,0:T(8,128)(2,1)S(1)}, bf16[2,32,1536]{2,1,0:T(8,128)(2,1)S(1)}, bf16[2,32,1536]{2,1,0:T(8,128)(2,1)S(1)}, bf16[2,32,1536]{2,1,0...) custom-call(bf16[2,256,256]{2,1,0:T(8,128)(2,1)S(1)} %copy-done.1, ...), custom_call_target="tpu_custom_call" | custom-call | flops 603979776 | bytes 2097152 | tf_op jit(solution)/shard_map/middle/pallas_call | solution.py:142
  51.7 0.1 collective-permute-start.12
  51.8 0.4 collective-permute-start.13
  52.2 0.0 collective-permute-done.3.refs_0_
  52.2 2.2 %collective-permute-start.14 = (bf16[2,32,1536]{2,1,0:T(8,128)(2,1)S(1)}, bf16[2,32,1536]{2,1,0:T(8,128)(2,1)S(1)}, u32[]{:S(2)}, u32[]{:S(2)}) collective-permute-start(bf16[2,32,1536]{2,1,0:T(8,128)(2,1)S(1)} %get-tuple-element.67), channel_id=1, source_target_pairs={{0,12},{4,8},{8,4},{12,0},{1,13},{5,9},{9,5},{13,1},{2,14},{6,10},... | collective-permute-start | bytes 589832 | tf_op jit(solution)/shard_map/ppermute | solution.py:259
  54.4 3.8 %collective-permute-done.4.refs_1_ = bf16[2,32,1536]{2,1,0:T(8,128)(2,1)S(1)} collective-permute-done((bf16[2,32,1536]{2,1,0:T(8,128)(2,1)S(1)}, bf16[2,32,1536]{2,1,0:T(8,128)(2,1)S(1)}, u32[]{:S(2)}, u32[]{:S(2)}) %collective-permute-start.4) | collective-permute-done | bytes 196640 | tf_op jit(solution)/shard_map/ppermute | solution.py:259
  58.2 0.0 collective-permute-done.5.refs_2_
  58.2 0.0 copy-done
  58.2 0.4 left_terms.2
  58.6 0.8 %collective-permute-start.9 = (f32[1,3,64,256]{3,2,1,0:T(8,128)S(1)}, f32[1,3,64,256]{3,2,1,0:T(8,128)S(1)}, u32[]{:S(2)}, u32[]{:S(2)}) collective-permute-start(f32[1,3,64,256]{3,2,1,0:T(8,128)S(1)} %get-tuple-element.61), channel_id=1, source_target_pairs={{0,1},{1,0},{2,3},{3,2},{4,5},{5,4},{6,7},{7,6},{8,9},{9,8},{10,11... | collective-permute-start | bytes 589832 | tf_op jit(solution)/shard_map/ppermute | solution.py:259
  59.5 1.2 %collective-permute-start.10 = (f32[1,3,64,256]{3,2,1,0:T(8,128)S(1)}, f32[1,3,64,256]{3,2,1,0:T(8,128)S(1)}, u32[]{:S(2)}, u32[]{:S(2)}) collective-permute-start(f32[1,3,64,256]{3,2,1,0:T(8,128)S(1)} %get-tuple-element.62), channel_id=1, source_target_pairs={{0,2},{1,3},{2,0},{3,1},{4,6},{5,7},{6,4},{7,5},{8,10},{9,11},{10,... | collective-permute-start | bytes 589832 | tf_op jit(solution)/shard_map/ppermute | solution.py:259
  60.7 0.0 collective-permute-done.12.refs_0_
  60.7 0.5 collective-permute-start.11
  61.2 0.0 collective-permute-done.13.refs_1_
  61.2 12.6 %collective-permute-done.14.refs_2_ = bf16[2,32,1536]{2,1,0:T(8,128)(2,1)S(1)} collective-permute-done((bf16[2,32,1536]{2,1,0:T(8,128)(2,1)S(1)}, bf16[2,32,1536]{2,1,0:T(8,128)(2,1)S(1)}, u32[]{:S(2)}, u32[]{:S(2)}) %collective-permute-start.14) | collective-permute-done | bytes 196640 | tf_op jit(solution)/shard_map/ppermute | solution.py:259
  73.8 0.4 left_terms.3
  74.2 0.6 collective-permute-start.15
  74.7 1.0 %collective-permute-done.15.got_ref = f32[2,1,64,256]{3,2,1,0:T(8,128)S(1)} collective-permute-done((f32[2,1,64,256]{3,2,1,0:T(8,128)S(1)}, f32[2,1,64,256]{3,2,1,0:T(8,128)S(1)}, u32[]{:S(2)}, u32[]{:S(2)}) %collective-permute-start.15) | collective-permute-done | bytes 131104 | tf_op jit(solution)/shard_map/ppermute | solution.py:259
  75.7 0.0 collective-permute-done.9.refs_1_
  75.7 0.0 collective-permute-done.10.refs_2_
  75.7 0.0 collective-permute-done.11.refs_3_
  75.8 1.3 %collective-permute-start.16 = (f32[1,1,64,256]{3,2,1,0:T(8,128)S(1)}, f32[1,1,64,256]{3,2,1,0:T(8,128)S(1)}, u32[]{:S(2)}, u32[]{:S(2)}) collective-permute-start(f32[1,1,64,256]{3,2,1,0:T(8,128)S(1)} %get-tuple-element.73), channel_id=1, source_target_pairs={{0,2},{1,3},{2,0},{3,1},{4,6},{5,7},{6,4},{7,5},{8,10},{9,11},{10,... | collective-permute-start | bytes 196616 | tf_op jit(solution)/shard_map/ppermute | solution.py:259
  77.0 1.9 %collective-permute-done.16.refs_5_ = f32[1,1,64,256]{3,2,1,0:T(8,128)S(1)} collective-permute-done((f32[1,1,64,256]{3,2,1,0:T(8,128)S(1)}, f32[1,1,64,256]{3,2,1,0:T(8,128)S(1)}, u32[]{:S(2)}, u32[]{:S(2)}) %collective-permute-start.16) | collective-permute-done | bytes 65568 | tf_op jit(solution)/shard_map/ppermute | solution.py:259
  78.9 0.7 finish.1
  (1 shorter events, 0.0 us)
Async XLA Ops:
  0.6 23.6 %copy-start.1 = (bf16[2,256,256]{2,1,0:T(8,128)(2,1)S(1)}, bf16[2,256,256]{2,1,0:T(8,128)(2,1)}, u32[]{:S(2)}) copy-start(bf16[2,256,256]{2,1,0:T(8,128)(2,1)} %right_ref.2) | copy-start | bytes 786436
  2.7 12.2 %collective-permute-start = (bf16[2,32,1536]{2,1,0:T(8,128)(2,1)S(1)}, bf16[2,32,1536]{2,1,0:T(8,128)(2,1)S(1)}, u32[]{:S(2)}, u32[]{:S(2)}) collective-permute-start(bf16[2,32,1536]{2,1,0:T(8,128)(2,1)S(1)} %get-tuple-element.38), channel_id=1, source_target_pairs={{0,8},{4,12},{8,0},{12,4},{1,9},{5,13},{9,1},{13,5},{2,10},{6,14},... | collective-permute-start | bytes 589832 | tf_op jit(solution)/shard_map/ppermute | solution.py:259
  2.8 21.4 %collective-permute-start.1 = (bf16[2,32,1536]{2,1,0:T(8,128)(2,1)S(1)}, bf16[2,32,1536]{2,1,0:T(8,128)(2,1)S(1)}, u32[]{:S(2)}, u32[]{:S(2)}) collective-permute-start(bf16[2,32,1536]{2,1,0:T(8,128)(2,1)S(1)} %get-tuple-element.39), channel_id=1, source_target_pairs={{0,12},{4,8},{8,4},{12,0},{1,13},{5,9},{9,5},{13,1},{2,14},{6,10},... | collective-permute-start | bytes 589832 | tf_op jit(solution)/shard_map/ppermute | solution.py:259
  5.2 18.9 %collective-permute-start.2 = (bf16[2,32,1536]{2,1,0:T(8,128)(2,1)S(1)}, bf16[2,32,1536]{2,1,0:T(8,128)(2,1)S(1)}, u32[]{:S(2)}, u32[]{:S(2)}) collective-permute-start(bf16[2,32,1536]{2,1,0:T(8,128)(2,1)S(1)} %get-tuple-element.40), channel_id=1, source_target_pairs={{0,4},{4,0},{8,12},{12,8},{1,5},{5,1},{9,13},{13,9},{2,6},{6,2},{1... | collective-permute-start | bytes 589832 | tf_op jit(solution)/shard_map/ppermute | solution.py:259
  8.3 19.2 %collective-permute-start.6 = (bf16[2,32,1536]{2,1,0:T(8,128)(2,1)S(1)}, bf16[2,32,1536]{2,1,0:T(8,128)(2,1)S(1)}, u32[]{:S(2)}, u32[]{:S(2)}) collective-permute-start(bf16[2,32,1536]{2,1,0:T(8,128)(2,1)S(1)} %get-tuple-element.52), channel_id=1, source_target_pairs={{0,4},{4,0},{8,12},{12,8},{1,5},{5,1},{9,13},{13,9},{2,6},{6,2},{1... | collective-permute-start | bytes 589832 | tf_op jit(solution)/shard_map/ppermute | solution.py:259
  8.8 31.4 %collective-permute-start.7 = (bf16[2,32,1536]{2,1,0:T(8,128)(2,1)S(1)}, bf16[2,32,1536]{2,1,0:T(8,128)(2,1)S(1)}, u32[]{:S(2)}, u32[]{:S(2)}) collective-permute-start(bf16[2,32,1536]{2,1,0:T(8,128)(2,1)S(1)} %get-tuple-element.53), channel_id=1, source_target_pairs={{0,8},{4,12},{8,0},{12,4},{1,9},{5,13},{9,1},{13,5},{2,10},{6,14},... | collective-permute-start | bytes 589832 | tf_op jit(solution)/shard_map/ppermute | solution.py:259
  14.9 33.6 %collective-permute-start.8 = (bf16[2,32,1536]{2,1,0:T(8,128)(2,1)S(1)}, bf16[2,32,1536]{2,1,0:T(8,128)(2,1)S(1)}, u32[]{:S(2)}, u32[]{:S(2)}) collective-permute-start(bf16[2,32,1536]{2,1,0:T(8,128)(2,1)S(1)} %get-tuple-element.54), channel_id=1, source_target_pairs={{0,12},{4,8},{8,4},{12,0},{1,13},{5,9},{9,5},{13,1},{2,14},{6,10},... | collective-permute-start | bytes 589832 | tf_op jit(solution)/shard_map/ppermute | solution.py:259
  27.4 30.9 %copy-start = (bf16[1536,512]{1,0:T(8,128)(2,1)S(1)}, bf16[1536,512]{1,0:T(8,128)(2,1)}, u32[]{:S(2)}) copy-start(bf16[1536,512]{1,0:T(8,128)(2,1)} %x_ref.6) | copy-start | bytes 4718596
  27.4 24.8 %collective-permute-start.3 = (bf16[2,32,1536]{2,1,0:T(8,128)(2,1)S(1)}, bf16[2,32,1536]{2,1,0:T(8,128)(2,1)S(1)}, u32[]{:S(2)}, u32[]{:S(2)}) collective-permute-start(bf16[2,32,1536]{2,1,0:T(8,128)(2,1)S(1)} %get-tuple-element.42), channel_id=1, source_target_pairs={{0,8},{4,12},{8,0},{12,4},{1,9},{5,13},{9,1},{13,5},{2,10},{6,14},... | collective-permute-start | bytes 589832 | tf_op jit(solution)/shard_map/ppermute | solution.py:259
  27.5 30.8 %collective-permute-start.4 = (bf16[2,32,1536]{2,1,0:T(8,128)(2,1)S(1)}, bf16[2,32,1536]{2,1,0:T(8,128)(2,1)S(1)}, u32[]{:S(2)}, u32[]{:S(2)}) collective-permute-start(bf16[2,32,1536]{2,1,0:T(8,128)(2,1)S(1)} %get-tuple-element.43), channel_id=1, source_target_pairs={{0,12},{4,8},{8,4},{12,0},{1,13},{5,9},{9,5},{13,1},{2,14},{6,10},... | collective-permute-start | bytes 589832 | tf_op jit(solution)/shard_map/ppermute | solution.py:259
  27.5 30.7 %collective-permute-start.5 = (bf16[2,32,1536]{2,1,0:T(8,128)(2,1)S(1)}, bf16[2,32,1536]{2,1,0:T(8,128)(2,1)S(1)}, u32[]{:S(2)}, u32[]{:S(2)}) collective-permute-start(bf16[2,32,1536]{2,1,0:T(8,128)(2,1)S(1)} %get-tuple-element.44), channel_id=1, source_target_pairs={{0,4},{4,0},{8,12},{12,8},{1,5},{5,1},{9,13},{13,9},{2,6},{6,2},{1... | collective-permute-start | bytes 589832 | tf_op jit(solution)/shard_map/ppermute | solution.py:259
  51.7 9.0 %collective-permute-start.12 = (bf16[2,32,1536]{2,1,0:T(8,128)(2,1)S(1)}, bf16[2,32,1536]{2,1,0:T(8,128)(2,1)S(1)}, u32[]{:S(2)}, u32[]{:S(2)}) collective-permute-start(bf16[2,32,1536]{2,1,0:T(8,128)(2,1)S(1)} %get-tuple-element.65), channel_id=1, source_target_pairs={{0,4},{4,0},{8,12},{12,8},{1,5},{5,1},{9,13},{13,9},{2,6},{6,2},{1... | collective-permute-start | bytes 589832 | tf_op jit(solution)/shard_map/ppermute | solution.py:259
  51.8 9.5 %collective-permute-start.13 = (bf16[2,32,1536]{2,1,0:T(8,128)(2,1)S(1)}, bf16[2,32,1536]{2,1,0:T(8,128)(2,1)S(1)}, u32[]{:S(2)}, u32[]{:S(2)}) collective-permute-start(bf16[2,32,1536]{2,1,0:T(8,128)(2,1)S(1)} %get-tuple-element.66), channel_id=1, source_target_pairs={{0,8},{4,12},{8,0},{12,4},{1,9},{5,13},{9,1},{13,5},{2,10},{6,14},... | collective-permute-start | bytes 589832 | tf_op jit(solution)/shard_map/ppermute | solution.py:259
  52.2 21.6 %collective-permute-start.14 = (bf16[2,32,1536]{2,1,0:T(8,128)(2,1)S(1)}, bf16[2,32,1536]{2,1,0:T(8,128)(2,1)S(1)}, u32[]{:S(2)}, u32[]{:S(2)}) collective-permute-start(bf16[2,32,1536]{2,1,0:T(8,128)(2,1)S(1)} %get-tuple-element.67), channel_id=1, source_target_pairs={{0,12},{4,8},{8,4},{12,0},{1,13},{5,9},{9,5},{13,1},{2,14},{6,10},... | collective-permute-start | bytes 589832 | tf_op jit(solution)/shard_map/ppermute | solution.py:259
  58.6 17.1 %collective-permute-start.9 = (f32[1,3,64,256]{3,2,1,0:T(8,128)S(1)}, f32[1,3,64,256]{3,2,1,0:T(8,128)S(1)}, u32[]{:S(2)}, u32[]{:S(2)}) collective-permute-start(f32[1,3,64,256]{3,2,1,0:T(8,128)S(1)} %get-tuple-element.61), channel_id=1, source_target_pairs={{0,1},{1,0},{2,3},{3,2},{4,5},{5,4},{6,7},{7,6},{8,9},{9,8},{10,11... | collective-permute-start | bytes 589832 | tf_op jit(solution)/shard_map/ppermute | solution.py:259
  59.5 16.2 %collective-permute-start.10 = (f32[1,3,64,256]{3,2,1,0:T(8,128)S(1)}, f32[1,3,64,256]{3,2,1,0:T(8,128)S(1)}, u32[]{:S(2)}, u32[]{:S(2)}) collective-permute-start(f32[1,3,64,256]{3,2,1,0:T(8,128)S(1)} %get-tuple-element.62), channel_id=1, source_target_pairs={{0,2},{1,3},{2,0},{3,1},{4,6},{5,7},{6,4},{7,5},{8,10},{9,11},{10,... | collective-permute-start | bytes 589832 | tf_op jit(solution)/shard_map/ppermute | solution.py:259
  60.7 15.0 %collective-permute-start.11 = (f32[1,3,64,256]{3,2,1,0:T(8,128)S(1)}, f32[1,3,64,256]{3,2,1,0:T(8,128)S(1)}, u32[]{:S(2)}, u32[]{:S(2)}) collective-permute-start(f32[1,3,64,256]{3,2,1,0:T(8,128)S(1)} %get-tuple-element.63), channel_id=1, source_target_pairs={{0,3},{1,2},{2,1},{3,0},{4,7},{5,6},{6,5},{7,4},{8,11},{9,10},{10,... | collective-permute-start | bytes 589832 | tf_op jit(solution)/shard_map/ppermute | solution.py:259
  74.2 1.5 %collective-permute-start.15 = (f32[2,1,64,256]{3,2,1,0:T(8,128)S(1)}, f32[2,1,64,256]{3,2,1,0:T(8,128)S(1)}, u32[]{:S(2)}, u32[]{:S(2)}) collective-permute-start(f32[2,1,64,256]{3,2,1,0:T(8,128)S(1)} %get-tuple-element.70), channel_id=1, source_target_pairs={{0,1},{1,0},{2,3},{3,2},{4,5},{5,4},{6,7},{7,6},{8,9},{9,8},{10,11... | collective-permute-start | bytes 393224 | tf_op jit(solution)/shard_map/ppermute | solution.py:259
  75.8 3.2 %collective-permute-start.16 = (f32[1,1,64,256]{3,2,1,0:T(8,128)S(1)}, f32[1,1,64,256]{3,2,1,0:T(8,128)S(1)}, u32[]{:S(2)}, u32[]{:S(2)}) collective-permute-start(f32[1,1,64,256]{3,2,1,0:T(8,128)S(1)} %get-tuple-element.73), channel_id=1, source_target_pairs={{0,2},{1,3},{2,0},{3,1},{4,6},{5,7},{6,4},{7,5},{8,10},{9,11},{10,... | collective-permute-start | bytes 196616 | tf_op jit(solution)/shard_map/ppermute | solution.py:259

commit v4 on v3

--- a/solution.py
+++ b/solution.py
@@ -53,13 +53,14 @@
     blocks, width = left_ref.shape[0], left_ref.shape[1]
     rows = width // peers
     step = rows // blocks
-    tile = x_ref.shape[0] // tiles
+    tokens = x_ref.shape[0]
+    marks = [0, tokens // 3, tokens]
     me = lax.axis_index("blk")
     fetch = pltpu.make_async_copy(left_ref, whole_left, left_sem)
     fetch.start()
     loads = []
     for n in range(tiles):
-        at = pl.ds(n * tile, tile)
+        at = pl.ds(marks[n], marks[n + 1] - marks[n])
         loads.append(pltpu.make_async_copy(x_ref.at[at], rows_in.at[at], row_sems.at[n]))
         loads[-1].start()
     fetch.wait()
@@ -69,12 +70,12 @@
             held[k, d * step : (d + 1) * step, :] = whole_left[k, pl.ds(at, step), :]
     for n in range(tiles):
         loads[n].wait()
-        low = n * tile
-        for k in range(blocks):
-            part = rows_in[low : low + tile, k * width : (k + 1) * width]
+        low, high = marks[n], marks[n + 1]
+        for k in range(blocks):
+            part = rows_in[low:high, k * width : (k + 1) * width]
             first = dot(held[k], part, NT).astype(BF16)
             for d in range(peers):
-                outs[d][k, :, low : low + tile] = first[d * step : (d + 1) * step]
+                outs[d][k, :, low:high] = first[d * step : (d + 1) * step]
 
 
 def forward(left, x, peers, g, tiles):
@@ -215,37 +216,55 @@
     )(keep, got)
 
 
-def finish_kernel(counts, scale, *refs):
-    left_out, right_out = refs[sum(counts) :]
+def sum_kernel(count, scale, *refs):
+    parts, (rows_out, *right_out) = refs[:count], refs[count:]
+    last = parts[0].shape[1] - 1
+    for n in range(last + 1):
+        total = parts[0][0, n]
+        for p in parts[1:]:
+            total = total + p[0, n]
+        if n < last:
+            right_out[0][n] = total * scale
+        else:
+            rows_out[...] = total * scale
+
+
+def tok_sum(group, scale):
+    _, height, rows, width = group[0].shape
+    shapes = [jax.ShapeDtypeStruct((rows, width), F32)]
+    if height > 1:
+        shapes.append(jax.ShapeDtypeStruct((height - 1, rows, width), F32))
+    return call(
+        functools.partial(sum_kernel, len(group), scale),
+        "tok_sum",
+        1,
+        in_specs=[pl.BlockSpec(memory_space=pltpu.VMEM)] * len(group),
+        out_specs=[pl.BlockSpec(memory_space=pltpu.VMEM)] * len(shapes),
+        out_shape=shapes,
+    )(*group)
+
+
+def finish_kernel(scale, keep, got, *refs):
+    done, left_out = refs[:-1], refs[-1]
     blocks, rows, _ = left_out.shape
-    step = rows // len(counts)
-    for g, count in enumerate(counts):
-        parts, refs = refs[:count], refs[count:]
-        last = parts[0].shape[1] - 1
-        for n in range(last + 1):
-            total = parts[0][0, n]
-            for p in parts[1:]:
-                total = total + p[0, n]
-            total = total * scale
-            if n < last:
-                right_out[n] = total
-            else:
-                for k in range(blocks):
-                    left_out[k, g * step : (g + 1) * step, :] = total[k * step : (k + 1) * step]
-
-
-def finish(groups, blocks, scale):
-    _, _, rows, width = groups[0][0].shape
-    flat = [a for group in groups for a in group]
-    shape = jax.ShapeDtypeStruct((blocks, rows, width), F32)
-    return call(
-        functools.partial(finish_kernel, [len(group) for group in groups], scale),
+    step = rows // (len(done) + 1)
+    total = (keep[0, 0] + got[0, 0]) * scale
+    for k in range(blocks):
+        for g, ref in enumerate(done):
+            left_out[k, g * step : (g + 1) * step, :] = ref[k * step : (k + 1) * step, :]
+        left_out[k, rows - step :, :] = total[k * step : (k + 1) * step]
+
+
+def finish(keep, got, done, blocks, scale):
+    _, _, rows, width = keep.shape
+    return call(
+        functools.partial(finish_kernel, scale),
         "finish",
         1,
-        in_specs=[pl.BlockSpec(memory_space=pltpu.VMEM)] * len(flat),
-        out_specs=[pl.BlockSpec(memory_space=pltpu.VMEM)] * 2,
-        out_shape=[shape] * 2,
-    )(*flat)
+        in_specs=[pl.BlockSpec(memory_space=pltpu.VMEM)] * (2 + len(done)),
+        out_specs=pl.BlockSpec(memory_space=pltpu.VMEM),
+        out_shape=jax.ShapeDtypeStruct((blocks, rows, width), F32),
+    )(keep, got, *done)
 
 
 def on_device(inputs, targets, left_factor, right_factor):
@@ -253,7 +272,7 @@
     blocks = left_factor.shape[0]
     peers = lax.axis_size("blk")
     toks = lax.axis_size("tok")
-    tile = tokens // 3
+    tile = tokens // 2
 
     def swap(axis, size, d, value):
         return lax.ppermute(value, axis, [(j, j ^ d) for j in range(size)])
@@ -273,7 +292,10 @@
     for g in range(blocks):
         res = middle(right, targets, arrived[g], toks, g, tile)
         right = after(right_factor, *res[:peers])
-        returned.append(exchange("blk", res[:peers]))
+        sent = list(res[:peers])
+        if g:
+            sent[-1] = after(sent[-1], returned[0][-1])
+        returned.append(exchange("blk", sent))
         terms.append(res[peers:])
 
     rows, groups = inputs, []
@@ -289,10 +311,15 @@
             while hop < toks:
                 keep, send = fold(keep, got)
                 got, hop = swap("tok", toks, hop, send), 2 * hop
-            groups.append([keep, got])
         else:
             groups.append(exchange("tok", out))
-    return tuple(finish(groups, blocks, 1.0 / tokens))
+    scale = 1.0 / tokens
+    done, grad_right = [], None
+    for group in groups:
+        rows, *right = tok_sum(group, scale)
+        done.append(rows)
+        grad_right = right[0] if right else grad_right
+    return finish(keep, got, done, blocks, scale), grad_right
 
 
 def solution(mesh):

time: 80.8 us -> 80.6 us (level)
    pallas_call x2, Pallas kernels: 6.34 us -> 5.24 us  [middle(): call(functools.partial(middle_kernel, peers, toks, g, order), 'middle', 6...]
  transfers between devices with their start and end apart: 17 -> 17, of which waited for: 8 -> 9; matrix products, arithmetic and copies ran while one was open for 0% -> 0% of each run, Pallas kernels for 11% -> 11%
where the time goes in v4:
time: 80.6 us; the launch traced here: 79.6 us
  waiting for transfers between devices  47.7 us (59%)
  starting transfers between devices  19.8 us (25%)
  Pallas kernels  11.4 us (14%)
    ppermute x17, waiting for transfers between devices, swap(): return lax.ppermute(value, axis, [(j, j ^ d) for j in range(size)])  47.7 us
    ppermute x17, starting transfers between devices, swap(): return lax.ppermute(value, axis, [(j, j ^ d) for j in range(size)])  19.8 us
    pallas_call x2, Pallas kernels, middle(): call(functools.partial(middle_kernel, peers, toks, g, order), 'middle', 6...  5.24 us
    pallas_call x2, Pallas kernels, forward(): call(functools.partial(forward_kernel, peers, g, tiles), 'forward', 2 * t...  3.98 us
  transfers between devices with their start and end apart: 17, of which 9 were waited for; matrix products, arithmetic and copies ran while one was open for 0% of the time, Pallas kernels for 11%

profile of v4, /device:TPU:21, one launch (start us, length us, event | category | flops | bytes accessed | tf_op | source)
XLA Modules:
  0.0 79.6 jit_solution(5927041900307562420)
XLA Ops:
  0.6 0.0 copy-start.1
  0.6 2.0 %forward.2 = (bf16[2,32,1536]{2,1,0:T(8,128)(2,1)S(1)}, bf16[2,32,1536]{2,1,0:T(8,128)(2,1)S(1)}, bf16[2,32,1536]{2,1,0:T(8,128)(2,1)S(1)}, bf16[2,32,1536]{2,1,0:T(8,128)(2,1)S(1)}) custom-call(bf16[2,256,256]{2,1,0:T(8,128)(2,1)} %left_ref.2, bf16[1536,512]{1,0:T(8,128)(2,1)} %x_ref.6), custom_call_target="tpu_custom_call" | custom-call | flops 201326592 | bytes 1572864 | tf_op jit(solution)/shard_map/forward/pallas_call | solution.py:85
  2.7 0.1 collective-permute-start
  2.8 2.4 %collective-permute-start.1 = (bf16[2,32,1536]{2,1,0:T(8,128)(2,1)S(1)}, bf16[2,32,1536]{2,1,0:T(8,128)(2,1)S(1)}, u32[]{:S(2)}, u32[]{:S(2)}) collective-permute-start(bf16[2,32,1536]{2,1,0:T(8,128)(2,1)S(1)} %get-tuple-element.42), channel_id=1, source_target_pairs={{0,12},{4,8},{8,4},{12,0},{1,13},{5,9},{9,5},{13,1},{2,14},{6,10},... | collective-permute-start | bytes 589832 | tf_op jit(solution)/shard_map/ppermute | solution.py:278
  5.2 1.1 %collective-permute-start.2 = (bf16[2,32,1536]{2,1,0:T(8,128)(2,1)S(1)}, bf16[2,32,1536]{2,1,0:T(8,128)(2,1)S(1)}, u32[]{:S(2)}, u32[]{:S(2)}) collective-permute-start(bf16[2,32,1536]{2,1,0:T(8,128)(2,1)S(1)} %get-tuple-element.43), channel_id=1, source_target_pairs={{0,4},{4,0},{8,12},{12,8},{1,5},{5,1},{9,13},{13,9},{2,6},{6,2},{1... | collective-permute-start | bytes 589832 | tf_op jit(solution)/shard_map/ppermute | solution.py:278
  6.3 2.0 %forward.3 = (bf16[2,32,1536]{2,1,0:T(8,128)(2,1)S(1)}, bf16[2,32,1536]{2,1,0:T(8,128)(2,1)S(1)}, bf16[2,32,1536]{2,1,0:T(8,128)(2,1)S(1)}, bf16[2,32,1536]{2,1,0:T(8,128)(2,1)S(1)}) custom-call(bf16[2,256,256]{2,1,0:T(8,128)(2,1)} %left_ref.2, bf16[1536,512]{1,0:T(8,128)(2,1)} %x_ref.6), custom_call_target="tpu_custom_call" | custom-call | flops 201326592 | bytes 1572864 | tf_op jit(solution)/shard_map/forward/pallas_call | solution.py:85
  8.2 0.5 collective-permute-start.6
  8.7 1.0 %collective-permute-start.7 = (bf16[2,32,1536]{2,1,0:T(8,128)(2,1)S(1)}, bf16[2,32,1536]{2,1,0:T(8,128)(2,1)S(1)}, u32[]{:S(2)}, u32[]{:S(2)}) collective-permute-start(bf16[2,32,1536]{2,1,0:T(8,128)(2,1)S(1)} %get-tuple-element.56), channel_id=1, source_target_pairs={{0,8},{4,12},{8,0},{12,4},{1,9},{5,13},{9,1},{13,5},{2,10},{6,14},... | collective-permute-start | bytes 589832 | tf_op jit(solution)/shard_map/ppermute | solution.py:278
  9.7 5.1 %collective-permute-done.refs_0_ = bf16[2,32,1536]{2,1,0:T(8,128)(2,1)S(1)} collective-permute-done((bf16[2,32,1536]{2,1,0:T(8,128)(2,1)S(1)}, bf16[2,32,1536]{2,1,0:T(8,128)(2,1)S(1)}, u32[]{:S(2)}, u32[]{:S(2)}) %collective-permute-start) | collective-permute-done | bytes 196640 | tf_op jit(solution)/shard_map/ppermute | solution.py:278
  14.8 3.3 %collective-permute-start.8 = (bf16[2,32,1536]{2,1,0:T(8,128)(2,1)S(1)}, bf16[2,32,1536]{2,1,0:T(8,128)(2,1)S(1)}, u32[]{:S(2)}, u32[]{:S(2)}) collective-permute-start(bf16[2,32,1536]{2,1,0:T(8,128)(2,1)S(1)} %get-tuple-element.57), channel_id=1, source_target_pairs={{0,12},{4,8},{8,4},{12,0},{1,13},{5,9},{9,5},{13,1},{2,14},{6,10},... | collective-permute-start | bytes 589832 | tf_op jit(solution)/shard_map/ppermute | solution.py:278
  18.2 6.0 %collective-permute-done.1.refs_1_ = bf16[2,32,1536]{2,1,0:T(8,128)(2,1)S(1)} collective-permute-done((bf16[2,32,1536]{2,1,0:T(8,128)(2,1)S(1)}, bf16[2,32,1536]{2,1,0:T(8,128)(2,1)S(1)}, u32[]{:S(2)}, u32[]{:S(2)}) %collective-permute-start.1) | collective-permute-done | bytes 196640 | tf_op jit(solution)/shard_map/ppermute | solution.py:278
  24.1 0.0 collective-permute-done.2.refs_2_
  24.1 0.0 copy-done.1
  24.1 2.6 %middle.2 = (bf16[2,32,1536]{2,1,0:T(8,128)(2,1)S(1)}, bf16[2,32,1536]{2,1,0:T(8,128)(2,1)S(1)}, bf16[2,32,1536]{2,1,0:T(8,128)(2,1)S(1)}, bf16[2,32,1536]{2,1,0...) custom-call(bf16[2,256,256]{2,1,0:T(8,128)(2,1)S(1)} %copy-done.1, ...), custom_call_target="tpu_custom_call" | custom-call | flops 603979776 | bytes 2097152 | tf_op jit(solution)/shard_map/middle/pallas_call | solution.py:143
  26.8 0.0 copy-start
  26.8 0.1 collective-permute-start.4
  26.9 0.1 collective-permute-start.3
  26.9 0.0 collective-permute-done.6.refs_0_
  27.0 2.5 %collective-permute-start.5 = (bf16[2,32,1536]{2,1,0:T(8,128)(2,1)S(1)}, bf16[2,32,1536]{2,1,0:T(8,128)(2,1)S(1)}, u32[]{:S(2)}, u32[]{:S(2)}) collective-permute-start(bf16[2,32,1536]{2,1,0:T(8,128)(2,1)S(1)} %get-tuple-element.47), channel_id=1, source_target_pairs={{0,4},{4,0},{8,12},{12,8},{1,5},{5,1},{9,13},{13,9},{2,6},{6,2},{1... | collective-permute-start | bytes 589832 | tf_op jit(solution)/shard_map/ppermute | solution.py:278
  29.5 10.7 %collective-permute-done.7.refs_1_ = bf16[2,32,1536]{2,1,0:T(8,128)(2,1)S(1)} collective-permute-done((bf16[2,32,1536]{2,1,0:T(8,128)(2,1)S(1)}, bf16[2,32,1536]{2,1,0:T(8,128)(2,1)S(1)}, u32[]{:S(2)}, u32[]{:S(2)}) %collective-permute-start.7) | collective-permute-done | bytes 196640 | tf_op jit(solution)/shard_map/ppermute | solution.py:278
  40.2 8.3 %collective-permute-done.8.refs_2_ = bf16[2,32,1536]{2,1,0:T(8,128)(2,1)S(1)} collective-permute-done((bf16[2,32,1536]{2,1,0:T(8,128)(2,1)S(1)}, bf16[2,32,1536]{2,1,0:T(8,128)(2,1)S(1)}, u32[]{:S(2)}, u32[]{:S(2)}) %collective-permute-start.8) | collective-permute-done | bytes 196640 | tf_op jit(solution)/shard_map/ppermute | solution.py:278
  48.5 2.6 %middle.3 = (bf16[2,32,1536]{2,1,0:T(8,128)(2,1)S(1)}, bf16[2,32,1536]{2,1,0:T(8,128)(2,1)S(1)}, bf16[2,32,1536]{2,1,0:T(8,128)(2,1)S(1)}, bf16[2,32,1536]{2,1,0...) custom-call(bf16[2,256,256]{2,1,0:T(8,128)(2,1)S(1)} %copy-done.1, ...), custom_call_target="tpu_custom_call" | custom-call | flops 603979776 | bytes 2097152 | tf_op jit(solution)/shard_map/middle/pallas_call | solution.py:143
  51.1 0.1 collective-permute-start.9
  51.2 0.4 collective-permute-start.10
  51.6 1.1 %collective-permute-done.4.refs_1_ = bf16[2,32,1536]{2,1,0:T(8,128)(2,1)S(1)} collective-permute-done((bf16[2,32,1536]{2,1,0:T(8,128)(2,1)S(1)}, bf16[2,32,1536]{2,1,0:T(8,128)(2,1)S(1)}, u32[]{:S(2)}, u32[]{:S(2)}) %collective-permute-start.4) | collective-permute-done | bytes 196640 | tf_op jit(solution)/shard_map/ppermute | solution.py:278
  52.7 1.1 %collective-permute-start.11 = (bf16[2,32,1536]{2,1,0:T(8,128)(2,1)S(1)}, bf16[2,32,1536]{2,1,0:T(8,128)(2,1)S(1)}, u32[]{:S(2)}, u32[]{:S(2)}) collective-permute-start(bf16[2,32,1536]{2,1,0:T(8,128)(2,1)S(1)} %get-tuple-element.71), channel_id=1, source_target_pairs={{0,12},{4,8},{8,4},{12,0},{1,13},{5,9},{9,5},{13,1},{2,14},{6,10},... | collective-permute-start | bytes 589832 | tf_op jit(solution)/shard_map/ppermute | solution.py:278
  53.8 0.0 collective-permute-done.3.refs_0_
  53.8 0.0 collective-permute-done.5.refs_2_
  53.8 0.0 copy-done
  53.8 0.4 left_terms.2
  54.2 1.8 %collective-permute-start.13 = (f32[1,3,64,256]{3,2,1,0:T(8,128)S(1)}, f32[1,3,64,256]{3,2,1,0:T(8,128)S(1)}, u32[]{:S(2)}, u32[]{:S(2)}) collective-permute-start(f32[1,3,64,256]{3,2,1,0:T(8,128)S(1)} %get-tuple-element.64), channel_id=1, source_target_pairs={{0,1},{1,0},{2,3},{3,2},{4,5},{5,4},{6,7},{7,6},{8,9},{9,8},{10,11... | collective-permute-start | bytes 589832 | tf_op jit(solution)/shard_map/ppermute | solution.py:278
  56.0 1.2 %collective-permute-start.14 = (f32[1,3,64,256]{3,2,1,0:T(8,128)S(1)}, f32[1,3,64,256]{3,2,1,0:T(8,128)S(1)}, u32[]{:S(2)}, u32[]{:S(2)}) collective-permute-start(f32[1,3,64,256]{3,2,1,0:T(8,128)S(1)} %get-tuple-element.65), channel_id=1, source_target_pairs={{0,2},{1,3},{2,0},{3,1},{4,6},{5,7},{6,4},{7,5},{8,10},{9,11},{10,... | collective-permute-start | bytes 589832 | tf_op jit(solution)/shard_map/ppermute | solution.py:278
  57.2 4.0 %collective-permute-done.9.refs_0_ = bf16[2,32,1536]{2,1,0:T(8,128)(2,1)S(1)} collective-permute-done((bf16[2,32,1536]{2,1,0:T(8,128)(2,1)S(1)}, bf16[2,32,1536]{2,1,0:T(8,128)(2,1)S(1)}, u32[]{:S(2)}, u32[]{:S(2)}) %collective-permute-start.9) | collective-permute-done | bytes 196640 | tf_op jit(solution)/shard_map/ppermute | solution.py:278
  61.2 2.2 %collective-permute-start.15 = (f32[1,3,64,256]{3,2,1,0:T(8,128)S(1)}, f32[1,3,64,256]{3,2,1,0:T(8,128)S(1)}, u32[]{:S(2)}, u32[]{:S(2)}) collective-permute-start(f32[1,3,64,256]{3,2,1,0:T(8,128)S(1)} %get-tuple-element.66), channel_id=1, source_target_pairs={{0,3},{1,2},{2,1},{3,0},{4,7},{5,6},{6,5},{7,4},{8,11},{9,10},{10,... | collective-permute-start | bytes 589832 | tf_op jit(solution)/shard_map/ppermute | solution.py:278
  63.5 0.0 collective-permute-done.10.refs_1_
  63.5 10.3 %collective-permute-done.11.refs_2_ = bf16[2,32,1536]{2,1,0:T(8,128)(2,1)S(1)} collective-permute-done((bf16[2,32,1536]{2,1,0:T(8,128)(2,1)S(1)}, bf16[2,32,1536]{2,1,0:T(8,128)(2,1)S(1)}, u32[]{:S(2)}, u32[]{:S(2)}) %collective-permute-start.11) | collective-permute-done | bytes 196640 | tf_op jit(solution)/shard_map/ppermute | solution.py:278
  73.8 0.4 left_terms.3
  74.2 0.6 collective-permute-start.12
  74.7 0.0 collective-permute-done.13.refs_1_
  74.7 0.0 collective-permute-done.14.refs_2_
  74.7 0.0 collective-permute-done.15.refs_3_
  74.8 1.0 %collective-permute-done.12.got_ref = f32[2,1,64,256]{3,2,1,0:T(8,128)S(1)} collective-permute-done((f32[2,1,64,256]{3,2,1,0:T(8,128)S(1)}, f32[2,1,64,256]{3,2,1,0:T(8,128)S(1)}, u32[]{:S(2)}, u32[]{:S(2)}) %collective-permute-start.12) | collective-permute-done | bytes 131104 | tf_op jit(solution)/shard_map/ppermute | solution.py:278
  75.7 1.3 %collective-permute-start.16 = (f32[1,1,64,256]{3,2,1,0:T(8,128)S(1)}, f32[1,1,64,256]{3,2,1,0:T(8,128)S(1)}, u32[]{:S(2)}, u32[]{:S(2)}) collective-permute-start(f32[1,1,64,256]{3,2,1,0:T(8,128)S(1)} %get-tuple-element.77), channel_id=1, source_target_pairs={{0,2},{1,3},{2,0},{3,1},{4,6},{5,7},{6,4},{7,5},{8,10},{9,11},{10,... | collective-permute-start | bytes 196616 | tf_op jit(solution)/shard_map/ppermute | solution.py:278
  77.0 0.7 tok_sum.1
  77.7 1.2 %collective-permute-done.16.got = f32[1,1,64,256]{3,2,1,0:T(8,128)S(1)} collective-permute-done((f32[1,1,64,256]{3,2,1,0:T(8,128)S(1)}, f32[1,1,64,256]{3,2,1,0:T(8,128)S(1)}, u32[]{:S(2)}, u32[]{:S(2)}) %collective-permute-start.16) | collective-permute-done | bytes 65568 | tf_op jit(solution)/shard_map/ppermute | solution.py:278
  78.9 0.7 finish.1
  (1 shorter events, 0.0 us)
Async XLA Ops:
  0.6 23.5 %copy-start.1 = (bf16[2,256,256]{2,1,0:T(8,128)(2,1)S(1)}, bf16[2,256,256]{2,1,0:T(8,128)(2,1)}, u32[]{:S(2)}) copy-start(bf16[2,256,256]{2,1,0:T(8,128)(2,1)} %right_ref.2) | copy-start | bytes 786436
  2.7 12.2 %collective-permute-start = (bf16[2,32,1536]{2,1,0:T(8,128)(2,1)S(1)}, bf16[2,32,1536]{2,1,0:T(8,128)(2,1)S(1)}, u32[]{:S(2)}, u32[]{:S(2)}) collective-permute-start(bf16[2,32,1536]{2,1,0:T(8,128)(2,1)S(1)} %get-tuple-element.41), channel_id=1, source_target_pairs={{0,8},{4,12},{8,0},{12,4},{1,9},{5,13},{9,1},{13,5},{2,10},{6,14},... | collective-permute-start | bytes 589832 | tf_op jit(solution)/shard_map/ppermute | solution.py:278
  2.8 21.4 %collective-permute-start.1 = (bf16[2,32,1536]{2,1,0:T(8,128)(2,1)S(1)}, bf16[2,32,1536]{2,1,0:T(8,128)(2,1)S(1)}, u32[]{:S(2)}, u32[]{:S(2)}) collective-permute-start(bf16[2,32,1536]{2,1,0:T(8,128)(2,1)S(1)} %get-tuple-element.42), channel_id=1, source_target_pairs={{0,12},{4,8},{8,4},{12,0},{1,13},{5,9},{9,5},{13,1},{2,14},{6,10},... | collective-permute-start | bytes 589832 | tf_op jit(solution)/shard_map/ppermute | solution.py:278
  5.2 18.9 %collective-permute-start.2 = (bf16[2,32,1536]{2,1,0:T(8,128)(2,1)S(1)}, bf16[2,32,1536]{2,1,0:T(8,128)(2,1)S(1)}, u32[]{:S(2)}, u32[]{:S(2)}) collective-permute-start(bf16[2,32,1536]{2,1,0:T(8,128)(2,1)S(1)} %get-tuple-element.43), channel_id=1, source_target_pairs={{0,4},{4,0},{8,12},{12,8},{1,5},{5,1},{9,13},{13,9},{2,6},{6,2},{1... | collective-permute-start | bytes 589832 | tf_op jit(solution)/shard_map/ppermute | solution.py:278
  8.2 18.7 %collective-permute-start.6 = (bf16[2,32,1536]{2,1,0:T(8,128)(2,1)S(1)}, bf16[2,32,1536]{2,1,0:T(8,128)(2,1)S(1)}, u32[]{:S(2)}, u32[]{:S(2)}) collective-permute-start(bf16[2,32,1536]{2,1,0:T(8,128)(2,1)S(1)} %get-tuple-element.55), channel_id=1, source_target_pairs={{0,4},{4,0},{8,12},{12,8},{1,5},{5,1},{9,13},{13,9},{2,6},{6,2},{1... | collective-permute-start | bytes 589832 | tf_op jit(solution)/shard_map/ppermute | solution.py:278
  8.7 31.4 %collective-permute-start.7 = (bf16[2,32,1536]{2,1,0:T(8,128)(2,1)S(1)}, bf16[2,32,1536]{2,1,0:T(8,128)(2,1)S(1)}, u32[]{:S(2)}, u32[]{:S(2)}) collective-permute-start(bf16[2,32,1536]{2,1,0:T(8,128)(2,1)S(1)} %get-tuple-element.56), channel_id=1, source_target_pairs={{0,8},{4,12},{8,0},{12,4},{1,9},{5,13},{9,1},{13,5},{2,10},{6,14},... | collective-permute-start | bytes 589832 | tf_op jit(solution)/shard_map/ppermute | solution.py:278
  14.8 33.6 %collective-permute-start.8 = (bf16[2,32,1536]{2,1,0:T(8,128)(2,1)S(1)}, bf16[2,32,1536]{2,1,0:T(8,128)(2,1)S(1)}, u32[]{:S(2)}, u32[]{:S(2)}) collective-permute-start(bf16[2,32,1536]{2,1,0:T(8,128)(2,1)S(1)} %get-tuple-element.57), channel_id=1, source_target_pairs={{0,12},{4,8},{8,4},{12,0},{1,13},{5,9},{9,5},{13,1},{2,14},{6,10},... | collective-permute-start | bytes 589832 | tf_op jit(solution)/shard_map/ppermute | solution.py:278
  26.8 27.0 %copy-start = (bf16[1536,512]{1,0:T(8,128)(2,1)S(1)}, bf16[1536,512]{1,0:T(8,128)(2,1)}, u32[]{:S(2)}) copy-start(bf16[1536,512]{1,0:T(8,128)(2,1)} %x_ref.6) | copy-start | bytes 4718596
  26.8 25.9 %collective-permute-start.4 = (bf16[2,32,1536]{2,1,0:T(8,128)(2,1)S(1)}, bf16[2,32,1536]{2,1,0:T(8,128)(2,1)S(1)}, u32[]{:S(2)}, u32[]{:S(2)}) collective-permute-start(bf16[2,32,1536]{2,1,0:T(8,128)(2,1)S(1)} %get-tuple-element.46), channel_id=1, source_target_pairs={{0,12},{4,8},{8,4},{12,0},{1,13},{5,9},{9,5},{13,1},{2,14},{6,10},... | collective-permute-start | bytes 589832 | tf_op jit(solution)/shard_map/ppermute | solution.py:278
  26.9 26.9 %collective-permute-start.3 = (bf16[2,32,1536]{2,1,0:T(8,128)(2,1)S(1)}, bf16[2,32,1536]{2,1,0:T(8,128)(2,1)S(1)}, u32[]{:S(2)}, u32[]{:S(2)}) collective-permute-start(bf16[2,32,1536]{2,1,0:T(8,128)(2,1)S(1)} %get-tuple-element.45), channel_id=1, source_target_pairs={{0,8},{4,12},{8,0},{12,4},{1,9},{5,13},{9,1},{13,5},{2,10},{6,14},... | collective-permute-start | bytes 589832 | tf_op jit(solution)/shard_map/ppermute | solution.py:278
  27.0 26.8 %collective-permute-start.5 = (bf16[2,32,1536]{2,1,0:T(8,128)(2,1)S(1)}, bf16[2,32,1536]{2,1,0:T(8,128)(2,1)S(1)}, u32[]{:S(2)}, u32[]{:S(2)}) collective-permute-start(bf16[2,32,1536]{2,1,0:T(8,128)(2,1)S(1)} %get-tuple-element.47), channel_id=1, source_target_pairs={{0,4},{4,0},{8,12},{12,8},{1,5},{5,1},{9,13},{13,9},{2,6},{6,2},{1... | collective-permute-start | bytes 589832 | tf_op jit(solution)/shard_map/ppermute | solution.py:278
  51.1 10.2 %collective-permute-start.9 = (bf16[2,32,1536]{2,1,0:T(8,128)(2,1)S(1)}, bf16[2,32,1536]{2,1,0:T(8,128)(2,1)S(1)}, u32[]{:S(2)}, u32[]{:S(2)}) collective-permute-start(bf16[2,32,1536]{2,1,0:T(8,128)(2,1)S(1)} %get-tuple-element.68), channel_id=1, source_target_pairs={{0,4},{4,0},{8,12},{12,8},{1,5},{5,1},{9,13},{13,9},{2,6},{6,2},{1... | collective-permute-start | bytes 589832 | tf_op jit(solution)/shard_map/ppermute | solution.py:278
  51.2 12.3 %collective-permute-start.10 = (bf16[2,32,1536]{2,1,0:T(8,128)(2,1)S(1)}, bf16[2,32,1536]{2,1,0:T(8,128)(2,1)S(1)}, u32[]{:S(2)}, u32[]{:S(2)}) collective-permute-start(bf16[2,32,1536]{2,1,0:T(8,128)(2,1)S(1)} %get-tuple-element.69), channel_id=1, source_target_pairs={{0,8},{4,12},{8,0},{12,4},{1,9},{5,13},{9,1},{13,5},{2,10},{6,14},... | collective-permute-start | bytes 589832 | tf_op jit(solution)/shard_map/ppermute | solution.py:278
  52.7 21.1 %collective-permute-start.11 = (bf16[2,32,1536]{2,1,0:T(8,128)(2,1)S(1)}, bf16[2,32,1536]{2,1,0:T(8,128)(2,1)S(1)}, u32[]{:S(2)}, u32[]{:S(2)}) collective-permute-start(bf16[2,32,1536]{2,1,0:T(8,128)(2,1)S(1)} %get-tuple-element.71), channel_id=1, source_target_pairs={{0,12},{4,8},{8,4},{12,0},{1,13},{5,9},{9,5},{13,1},{2,14},{6,10},... | collective-permute-start | bytes 589832 | tf_op jit(solution)/shard_map/ppermute | solution.py:278
  54.2 20.5 %collective-permute-start.13 = (f32[1,3,64,256]{3,2,1,0:T(8,128)S(1)}, f32[1,3,64,256]{3,2,1,0:T(8,128)S(1)}, u32[]{:S(2)}, u32[]{:S(2)}) collective-permute-start(f32[1,3,64,256]{3,2,1,0:T(8,128)S(1)} %get-tuple-element.64), channel_id=1, source_target_pairs={{0,1},{1,0},{2,3},{3,2},{4,5},{5,4},{6,7},{7,6},{8,9},{9,8},{10,11... | collective-permute-start | bytes 589832 | tf_op jit(solution)/shard_map/ppermute | solution.py:278
  56.0 18.8 %collective-permute-start.14 = (f32[1,3,64,256]{3,2,1,0:T(8,128)S(1)}, f32[1,3,64,256]{3,2,1,0:T(8,128)S(1)}, u32[]{:S(2)}, u32[]{:S(2)}) collective-permute-start(f32[1,3,64,256]{3,2,1,0:T(8,128)S(1)} %get-tuple-element.65), channel_id=1, source_target_pairs={{0,2},{1,3},{2,0},{3,1},{4,6},{5,7},{6,4},{7,5},{8,10},{9,11},{10,... | collective-permute-start | bytes 589832 | tf_op jit(solution)/shard_map/ppermute | solution.py:278
  61.2 13.5 %collective-permute-start.15 = (f32[1,3,64,256]{3,2,1,0:T(8,128)S(1)}, f32[1,3,64,256]{3,2,1,0:T(8,128)S(1)}, u32[]{:S(2)}, u32[]{:S(2)}) collective-permute-start(f32[1,3,64,256]{3,2,1,0:T(8,128)S(1)} %get-tuple-element.66), channel_id=1, source_target_pairs={{0,3},{1,2},{2,1},{3,0},{4,7},{5,6},{6,5},{7,4},{8,11},{9,10},{10,... | collective-permute-start | bytes 589832 | tf_op jit(solution)/shard_map/ppermute | solution.py:278
  74.2 1.5 %collective-permute-start.12 = (f32[2,1,64,256]{3,2,1,0:T(8,128)S(1)}, f32[2,1,64,256]{3,2,1,0:T(8,128)S(1)}, u32[]{:S(2)}, u32[]{:S(2)}) collective-permute-start(f32[2,1,64,256]{3,2,1,0:T(8,128)S(1)} %get-tuple-element.74), channel_id=1, source_target_pairs={{0,1},{1,0},{2,3},{3,2},{4,5},{5,4},{6,7},{7,6},{8,9},{9,8},{10,11... | collective-permute-start | bytes 393224 | tf_op jit(solution)/shard_map/ppermute | solution.py:278
  75.7 3.2 %collective-permute-start.16 = (f32[1,1,64,256]{3,2,1,0:T(8,128)S(1)}, f32[1,1,64,256]{3,2,1,0:T(8,128)S(1)}, u32[]{:S(2)}, u32[]{:S(2)}) collective-permute-start(f32[1,1,64,256]{3,2,1,0:T(8,128)S(1)} %get-tuple-element.77), channel_id=1, source_target_pairs={{0,2},{1,3},{2,0},{3,1},{4,6},{5,7},{6,4},{7,5},{8,10},{9,11},{10,... | collective-permute-start | bytes 196616 | tf_op jit(solution)/shard_map/ppermute | solution.py:278
